TPU v7x, 32 devices: a whole 2x2x4 slice. The times are simulated.
32 devices in a mesh: chan: 2 (over core), face: 4 (over y, x), tile: 4 (over z).
Axes of the slice: x: 2, y: 2, z: 4, core: 2. Of those that a mesh axis runs over, the one named last changes fastest.
Arguments:
- field: bfloat16 [1, 128, 32, 4096], P(None, 'chan', 'tile', 'face'), may hold values from -6 to 6
- conv_weight: bfloat16 [3, 3, 128, 128], replicated, may hold values from -0.1875 to 0.1875
- order_map: int32 [2048], replicated, may hold values from 0 to 2047, each once
- legendre: bfloat16 [2048, 32, 2048], P(('chan', 'face', 'tile')), may hold values from -0.015625 to 0.015625
- spectral_weight: bfloat16 [2048, 128, 128], P(('face', 'tile')), may hold values from -0.5 to 0.5
Outputs:
- spectrum: bfloat16 [2048, 2, 1, 2048, 128], P('chan', None, None, ('face', 'tile'))
Inputs may be any that keep to these rules, and one draw needn't show every extreme that they name: `order_map`: a permutation of the orders 0 to 2047.
All inputs are finite; a program needn't handle non-finite values.
Results may differ from a plain program's by a relative error of at most 0.013.
Values may be sent and summed in bfloat16 or wider, within the bound.
No kernel may reach another device: no remote copies, remote signals or barrier semaphores. Data moves between devices by JAX's collectives and lax.ppermute only.
A program may use at most 320 MiB of HBM per device.

v0:
```python
import math

import jax
import jax.numpy as jnp
from jax import lax
from jax.sharding import PartitionSpec as P


def extended(x, sides, width):
    for axis, dim in sides:
        count, length = (lax.axis_size(axis), x.shape[dim])
        up = [(i, (i + 1) % count) for i in range(count)]
        down = [(j, i) for i, j in up]
        last = lax.slice_in_dim(x, length - width, length, axis=dim)
        first = lax.slice_in_dim(x, 0, width, axis=dim)
        before = lax.ppermute(last, axis, up)
        after = lax.ppermute(first, axis, down)
        x = jnp.concatenate([before, x, after], axis=dim)
    return x


def stencil(padded, weights, cycle_count, pix_count):
    summed = None
    for shift_r in range(3):
        for shift_p in range(3):
            window = padded[:, :, shift_r : shift_r + cycle_count, shift_p : shift_p + pix_count]
            contrib = jnp.einsum(
                "birp,io->borp",
                window,
                weights[shift_r, shift_p],
                preferred_element_type=jnp.float32,
            )
            summed = contrib if summed is None else summed + contrib
    return summed


def clear_band_edges(padded, tile_id, tile_count):
    cycle_ids = jnp.arange(padded.shape[2], dtype=jnp.int32)
    at_start = (cycle_ids == 0) & (tile_id == 0)
    at_finish = (cycle_ids == padded.shape[2] - 1) & (tile_id == tile_count - 1)
    keeping = jnp.logical_not(at_start | at_finish)
    return jnp.where(keeping[None, None, :, None], padded, jnp.zeros_like(padded))


def twiddle_parts(orders, first_pixel, pix_count, pixels, parity):
    pixel_ids = first_pixel + jnp.arange(pix_count, dtype=jnp.int32)
    turns = orders[:, None] * (2 * pixel_ids[None, :] + parity) % (2 * pixels)
    angle = turns.astype(jnp.float32) * (math.pi / pixels)
    table = jnp.stack([jnp.cos(angle), -jnp.sin(angle)], axis=1)
    coarse = table.astype(jnp.bfloat16)
    finer = (table - coarse.astype(jnp.float32)).astype(jnp.bfloat16)
    return (coarse, finer)


def cycle_spectrum(cycle_rows, coarse, finer):
    first_part = jnp.einsum("kzp,np->kzn", coarse, cycle_rows, preferred_element_type=jnp.float32)
    second_part = jnp.einsum("kzp,np->kzn", finer, cycle_rows, preferred_element_type=jnp.float32)
    return first_part + second_part


def body(field, conv_weight, order_map, legendre, spectral_weight):
    n_chan = lax.axis_size("chan")
    n_face = lax.axis_size("face")
    n_tile = lax.axis_size("tile")
    chan_id = lax.axis_index("chan")
    face_id = lax.axis_index("face")
    tile_id = lax.axis_index("tile")
    samples, chan_dev, cycle_dev, pix_dev = field.shape
    channels = chan_dev * n_chan
    pixels = pix_dev * n_face
    degrees = legendre.shape[2]
    cycles = legendre.shape[1]
    slot_dev = legendre.shape[0]
    gathered = lax.all_gather(field, "chan", axis=1, tiled=True)
    padded = extended(gathered, (("face", 3), ("tile", 2)), 1)
    padded = clear_band_edges(padded, tile_id, n_tile)
    own_weight = lax.dynamic_slice_in_dim(conv_weight, chan_id * chan_dev, chan_dev, 3)
    hidden = stencil(padded, own_weight, cycle_dev, pix_dev).astype(jnp.bfloat16)
    rows_face = degrees // n_face
    per_chan = rows_face // n_chan
    row_ids = jnp.arange(lax.axis_size("face") * rows_face, dtype=jnp.int32)
    face_of = row_ids // rows_face
    within = row_ids % rows_face
    chan_of = within // per_chan
    within = within % per_chan
    tile_of = within // slot_dev
    offset = within % slot_dev
    slot_ids = ((chan_of * n_face + face_of) * n_tile + tile_of) * slot_dev + offset
    orders = jnp.take(order_map, slot_ids)
    halves = []
    for parity in range(2):
        cycle_rows = hidden[:, :, parity::2, :].reshape(-1, pix_dev)
        coarse, finer = twiddle_parts(orders, face_id * pix_dev, pix_dev, pixels, parity)
        halves.append(
            cycle_spectrum(cycle_rows, coarse, finer).reshape(
                lax.axis_size("face") * rows_face, 2, samples, chan_dev, cycle_dev // 2
            )
        )
    summed_terms = lax.psum_scatter(
        jnp.stack(halves, axis=-1).reshape(
            lax.axis_size("face") * rows_face, 2, samples, chan_dev, cycle_dev
        ),
        "face",
        scatter_dimension=0,
        tiled=True,
    ).astype(jnp.bfloat16)
    coeffs = lax.all_to_all(
        lax.all_to_all(summed_terms, "chan", split_axis=0, concat_axis=3, tiled=True),
        "tile",
        split_axis=0,
        concat_axis=4,
        tiled=True,
    )
    slot_start = ((chan_id * n_face + face_id) * n_tile + tile_id) * slot_dev
    own_orders = lax.dynamic_slice_in_dim(order_map, slot_start, slot_dev)
    mixed_rows = coeffs.reshape(slot_dev, 2 * samples * channels, cycles)
    degree_ids = jnp.arange(degrees, dtype=jnp.int32)
    assoc = jnp.einsum("kxr,krl->kxl", mixed_rows, legendre, preferred_element_type=jnp.float32)
    keeping = degree_ids[None, :] >= own_orders[:, None]
    assoc = jnp.where(keeping[:, None, :], assoc, jnp.zeros_like(assoc))
    assoc = assoc.astype(jnp.bfloat16).reshape(slot_dev, 2, samples, channels, degrees)
    filtered = jnp.einsum(
        "kzbil,lio->kzblo",
        lax.all_to_all(assoc, ("face", "tile"), split_axis=4, concat_axis=0, tiled=True),
        spectral_weight,
        preferred_element_type=jnp.float32,
    )
    return filtered.astype(jnp.bfloat16)


def solution(mesh):
    in_specs = (
        P(None, "chan", "tile", "face"),
        P(),
        P(),
        P(("chan", "face", "tile"), None, None),
        P(("face", "tile"), None, None),
    )
    out_specs = P("chan", None, None, ("face", "tile"), None)
    return jax.shard_map(body, mesh=mesh, in_specs=in_specs, out_specs=out_specs, check_vma=False)
```

profile of v0, /device:TPU:0, one launch (start us, length us, event | category | flops | bytes accessed | tf_op | source)
XLA Modules:
  0.0 2119.8 jit_solution(5118104642781468619)
XLA Ops:
  6.5 2.8 copy.50
  9.5 11.8 gather_fusion
  21.4 1.5 all-gather.2.cloned.1.call-done
  22.8 1.2 fusion.71
  24.0 2.7 collective-permute-start.1
  26.7 0.6 add_multiply_fusion
  27.3 6.1 collective-permute-done.1
  33.4 6.0 collective-permute-done
  39.4 4.8 concatenate.14
  44.2 0.8 fusion.70
  45.0 1.5 collective-permute-start.2
  46.5 2.8 collective-permute-start.3
  49.3 71.9 %fusion.16 = (f32[2048,1,1024]{2,0,1:T(8,128)}, f32[2048,1,1024]{2,0,1:T(8,128)}, f32[2048,1,1024]{2,0,1:T(8,128)}, f32[2048,1,1024]{2,0,1:T(8,128)}) fusion(s32[1024]{0:T(1024)} %get-tuple-element.17, s32[2048]{0:T(1024)S(1)} %and_select_fusion.6, s32[1024]{0:T(1024)} %get-tuple-element.18), kind=kLoop, calls=%fused_computation.34 | loop fusion | flops 62914560 | bytes 33570816 | tf_op jit(solution)/shard_map/cos | solution.py:49
  121.3 0.6 maximum_select_fusion
  121.9 0.5 fusion.21
  122.5 0.9 fusion.20
  123.3 0.9 fusion.22
  124.2 0.9 fusion.23
  125.1 0.6 fusion.24
  125.7 0.9 fusion.26
  126.5 0.9 fusion.25
  128.0 1.5 fusion.28
  130.6 7.4 fusion.2
  138.0 10.3 fusion.18
  148.2 5.2 stack_reshape.6
  153.4 6.7 copy.53
  160.1 7.3 fusion.4
  167.5 0.9 slice-done.3
  168.4 4.0 fusion.17
  172.4 5.2 stack_reshape.7
  177.6 4.8 copy.54
  182.3 4.0 pad_maximum_fusion.2
  186.3 84.7 %reduce-scatter.2.cloned.1.call-done = f32[512,2,1,64,8]{0,3,4,1,2:T(8,128)} async-done(((f32[2048,2,1,64,8]{0,3,4,1,2:T(8,128)}), f32[512,2,1,64,8]{0,3,4,1,2:T(8,128)}) %reduce-scatter.2.cloned.1.call-update) | async-done | bytes 2097168 | tf_op jit(solution)/shard_map/reduce_scatter | solution.py:99
  271.0 1.7 convert_element_type.80
  272.8 2.2 copy.55
  275.0 1.7 reshape.655
  276.7 5.4 all_to_all.48
  282.1 2.6 reshape.656
  284.7 2.7 copy.64
  287.6 2.0 copy.58
  289.6 4.6 all-to-all-start.1
  294.4 25.8 %all-to-all-done.1 = bf16[256,2,1,128,8]{3,4,2,1,0:T(8,128)(2,1)S(1)} async-done(((bf16[256,2,1,128,8]{3,4,2,1,0:T(8,128)(2,1)}), bf16[256,2,1,128,8]{3,4,2,1,0:T(8,128)(2,1)S(1)}, u32[]{:S(2)}, u32[]{:S(2)}) %all-to-all-start.1) | async-done | bytes 1048608 | tf_op jit(solution)/shard_map/all_to_all | solution.py:107
  320.2 28.5 %select_convert_fusion = bf16[64,256,2048]{2,1,0:T(8,128)(2,1)} fusion(pred[64,2048]{1,0:T(8,128)(4,1)S(1)} %iota_compare_fusion, bf16[64,32,2048]{2,1,0:T(8,128)(2,1)} %param.8, bf16[64,2,1,128,4,8]{3,5,2,1,0,4:T(8,128)(2,1)S(1)} %bitcast.135), kind=kOutput, calls=%fused_computation.1 | convolution fusion | flops 2214592512 | bytes 76677120 | tf_op jit(solution)/shard_map/kxr,krl->kxl/dot_general | solution.py:118
  348.8 161.8 %copy.60 = bf16[64,2,1,128,2048]{3,1,0,2,4:T(2,128)(2,1)} copy(bf16[64,2,1,128,2048]{4,3,1,0,2:T(8,128)(2,1)} %bitcast.36) | data formatting | bytes 134217728 | tf_op jit(solution)/shard_map/reshape | solution.py:121
  510.6 1454.2 %all_to_all.49 = bf16[64,2,1,128,2048]{3,1,0,2,4:T(2,128)(2,1)} all-to-all(bf16[64,2,1,128,2048]{3,1,0,2,4:T(2,128)(2,1)} %copy.60), channel_id=1, replica_groups=mesh['chan'=2,'face'=4,'tile'=4] {'face','tile'}, dimensions={4} | all-to-all | bytes 134217728 | tf_op jit(solution)/shard_map/all_to_all | solution.py:124
  1964.8 44.5 %copy.61 = bf16[64,2,1,128,16,128]{3,0,4,1,5,2:T(8,128)(2,1)} copy(bf16[64,2,1,128,16,128]{3,1,0,5,4,2:T(2,128)(2,1)} %bitcast.37) | data formatting | bytes 134217728 | tf_op jit(solution)/shard_map/all_to_all | solution.py:124
  2009.3 47.4 %convert_bitcast_fusion = bf16[1024,2,1,128,128]{4,0,1,3,2:T(8,128)(2,1)} fusion(bf16[1024,2,128,128]{2,0,1,3:T(8,128)(2,1)} %bitcast.39, bf16[128,128,128]{2,1,0:T(8,128)(2,1)} %param.9), kind=kOutput, calls=%fused_computation.2 | convolution fusion | flops 8623489024 | bytes 138412032 | tf_op jit(solution)/shard_map/kzbil,lio->kzblo/dot_general | solution.py:122
  2056.7 56.0 %copy.62 = bf16[1024,2,1,128,128]{4,3,2,1,0:T(8,128)(2,1)} copy(bf16[1024,2,1,128,128]{4,0,1,3,2:T(8,128)(2,1)} %convert_bitcast_fusion) | data formatting | bytes 134217728 | tf_op jit(solution)/shard_map/convert_element_type | solution.py:128
  (37 shorter events, 2.3 us)
Async XLA Ops:
  6.5 115.4 %copy-start = (bf16[3,3,128,128]{3,2,1,0:T(8,128)(2,1)S(1)}, bf16[3,3,128,128]{3,2,1,0:T(8,128)(2,1)}, u32[]{:S(2)}) copy-start(bf16[3,3,128,128]{3,2,1,0:T(8,128)(2,1)} %param.6) | copy-start | bytes 884740
  6.5 3.0 copy-start.2
  6.5 16.3 all-gather.2.cloned.1.call-start
  9.4 261.6 %reduce-scatter.2.cloned.1.call-start = ((), (), s32[]{:S(2)}) async-start(), calls=%async_computation.5 | async-start | bytes 10485760 | tf_op jit(solution)/shard_map/reduce_scatter | solution.py:99
  24.0 9.4 collective-permute-start.1
  26.7 12.6 collective-permute-start
  45.0 76.3 %collective-permute-start.2 = (bf16[1,128,1,1026]{3,1,2,0:T(8,128)(2,1)}, bf16[1,128,1,1026]{3,1,2,0:T(8,128)(2,1)S(1)}, u32[]{:S(2)}, u32[]{:S(2)}) collective-permute-start(bf16[1,128,1,1026]{3,1,2,0:T(8,128)(2,1)} %get-tuple-element.5), channel_id=1, source_target_pairs={{0,1},{1,2},{2,3},{3,0},{4,5},{5,6},{6,7},{7,4},{8,9},{9,10},{10,1... | collective-permute-start | bytes 787976 | tf_op jit(solution)/shard_map/ppermute | solution.py:16
  46.5 74.8 %collective-permute-start.3 = (bf16[1,128,1,1026]{3,1,2,0:T(8,128)(2,1)S(1)}, bf16[1,128,1,1026]{3,1,2,0:T(8,128)(2,1)S(1)}, u32[]{:S(2)}, u32[]{:S(2)}) collective-permute-start(bf16[1,128,1,1026]{3,1,2,0:T(8,128)(2,1)S(1)} %get-tuple-element.6), channel_id=1, source_target_pairs={{1,0},{2,1},{3,2},{0,3},{5,4},{6,5},{7,6},{4,7},{9,8},{10,9},{11,1... | collective-permute-start | bytes 787976 | tf_op jit(solution)/shard_map/ppermute | solution.py:17
  153.4 14.0 slice-start
  153.4 14.0 slice-start.2
  160.1 7.3 slice-start.1
  160.1 8.3 slice-start.3
  177.6 4.8 copy-start.3
  289.6 30.6 %all-to-all-start.1 = ((bf16[256,2,1,128,8]{3,4,2,1,0:T(8,128)(2,1)}), bf16[256,2,1,128,8]{3,4,2,1,0:T(8,128)(2,1)S(1)}, u32[]{:S(2)}, u32[]{:S(2)}) async-start(bf16[256,2,1,128,8]{3,4,2,1,0:T(8,128)(2,1)} %copy.58), calls=%async_computation.2 | async-start | bytes 2097152 | tf_op jit(solution)/shard_map/all_to_all | solution.py:107
  2056.7 56.0 %copy-start.1 = (bf16[3,3,128,128]{3,2,1,0:T(8,128)(2,1)S(1)}, bf16[3,3,128,128]{3,2,1,0:T(8,128)(2,1)}, u32[]{:S(2)}) copy-start(bf16[3,3,128,128]{3,2,1,0:T(8,128)(2,1)} %param.6) | copy-start | bytes 884740
Sparse Core Ops, SparseCore 0:
  9.5 13.2 all-gather.1
  186.5 84.5 reduce-scatter.1
where the time goes:
time: 2130 us; the launch traced here: 2120 us
  blocking collectives  1460 us (69%)
  local copies, waits for them, and re-layouts  319 us (15%)
  waiting for transfers between devices  124 us (6%)
  matrix products  112 us (5%)
  other arithmetic  79 us (4%)
    all_to_all x1, blocking collectives, body(): lax.all_to_all(assoc, ('face', 'tile'), split_axis=4, concat_axis=0, tile...  1450 us
    reshape x1, local copies, waits for them, and re-layouts, body(): assoc.astype(jnp.bfloat16).reshape(slot_dev, 2, samples, channels, degrees)  162 us
    reduce_scatter x1, waiting for transfers between devices, body(): lax.psum_scatter(jnp.stack(halves, axis=-1).reshape(lax.axis_size('face')...  84.7 us
    cos x1, other arithmetic, twiddle_parts(): table = jnp.stack([jnp.cos(angle), -jnp.sin(angle)], axis=1)  71.9 us
    convert_element_type x1, local copies, waits for them, and re-layouts, body(): return filtered.astype(jnp.bfloat16)  56 us
    dot_general x1, matrix products, body(): jnp.einsum('kzbil,lio->kzblo', lax.all_to_all(assoc, ('face', 'tile'), sp...  47.4 us
    all_to_all x1, local copies, waits for them, and re-layouts, body(): lax.all_to_all(assoc, ('face', 'tile'), split_axis=4, concat_axis=0, tile...  44.5 us
  transfers between devices with their start and end apart: 7, of which 5 were waited for; matrix products, arithmetic and copies ran while one was open for 4% of the time, Pallas kernels for 0%

commit v1 on v0

v1 whole, which is shorter than its diff:
```python
import functools
import math

import jax
import jax.numpy as jnp
from jax import lax
from jax.experimental import pallas as pl
from jax.experimental.pallas import tpu as pltpu
from jax.sharding import PartitionSpec as P

LANES = 128
ROWS = 8


def extended(x, sides, width):
    for axis, dim in sides:
        count, length = (lax.axis_size(axis), x.shape[dim])
        up = [(i, (i + 1) % count) for i in range(count)]
        down = [(j, i) for i, j in up]
        last = lax.slice_in_dim(x, length - width, length, axis=dim)
        first = lax.slice_in_dim(x, 0, width, axis=dim)
        before = lax.ppermute(last, axis, up)
        after = lax.ppermute(first, axis, down)
        x = jnp.concatenate([before, x, after], axis=dim)
    return x


def stencil(padded, weights, cycle_count, pix_count):
    summed = None
    for shift_r in range(3):
        for shift_p in range(3):
            window = padded[:, :, shift_r : shift_r + cycle_count, shift_p : shift_p + pix_count]
            contrib = jnp.einsum(
                "birp,io->borp",
                window,
                weights[shift_r, shift_p],
                preferred_element_type=jnp.float32,
            )
            summed = contrib if summed is None else summed + contrib
    return summed


def clear_band_edges(padded, tile_id, tile_count):
    cycle_ids = jnp.arange(padded.shape[2], dtype=jnp.int32)
    at_start = (cycle_ids == 0) & (tile_id == 0)
    at_finish = (cycle_ids == padded.shape[2] - 1) & (tile_id == tile_count - 1)
    keeping = jnp.logical_not(at_start | at_finish)
    return jnp.where(keeping[None, None, :, None], padded, jnp.zeros_like(padded))


def unit(turns, period):
    angle = (turns % (2 * period)).astype(jnp.float32) * (math.pi / period)
    return jnp.cos(angle), -jnp.sin(angle)


def cycle_spectrum(rows, parity, pixels, orders):
    parts, n_r, n_x, pix = rows.shape
    count = pixels // LANES
    tops = orders // count
    a = jnp.arange(count, dtype=jnp.int32)
    m1 = jnp.arange(count, dtype=jnp.int32)
    k = jnp.arange(tops, dtype=jnp.int32)
    half = 2 * jnp.arange(LANES, dtype=jnp.int32)[None, :] + parity[:, None]
    first = jnp.stack(unit(2 * m1[:, None] * a[None, :], count))
    first = first.reshape(2, count, parts, pix // LANES)
    x = rows.reshape(parts, n_r, n_x, pix // LANES, LANES).astype(jnp.float32)
    y = jnp.einsum("zmfa,frxab->zmrxb", first, x, precision=lax.Precision.HIGHEST)
    tw_re, tw_im = unit(m1[:, None, None] * half[None], pixels)
    tw_re, tw_im = tw_re[:, :, None], tw_im[:, :, None]
    turned = jnp.stack([y[0] * tw_re - y[1] * tw_im, y[0] * tw_im + y[1] * tw_re])
    g_re, g_im = unit(half[:, :, None] * k[None, None, :], LANES)
    second = jnp.stack([jnp.stack([g_re, g_im]), jnp.stack([-g_im, g_re])])
    return jnp.einsum(
        "imrxb,izrbk->mkrzx", turned, second, precision=lax.Precision.HIGHEST
    ).astype(jnp.bfloat16)


def mix_body(slots, nz, sub, step, c_ref, q_ref, w_ref, o_ref, a_ref, t_ref):
    pk, pn, srcs, per, rr, ln = c_ref.shape
    depth = pk * rr
    count, ch = w_ref.shape[0], w_ref.shape[1]
    lane = lax.broadcasted_iota(jnp.int32, (1, ROWS, depth), 2)
    row = lax.broadcasted_iota(jnp.int32, (1, ROWS, depth), 1)
    own = (lane % ROWS) == row

    def associate(i, carry):
        held = []
        for h in range(2):
            g = 2 * i + h
            a, b = g // per, g % per
            rhs = [c_ref[:, n, a, b].reshape(depth, ln) for n in range(pn)]
            held.append((a, b, jnp.concatenate(rhs, axis=1)))
        for l0 in range(0, count, step):
            parts = []
            for a, b, rhs in held:
                q = q_ref[a, b, pl.ds(l0, step), :].astype(jnp.float32)
                d = jnp.where(own, q[:, None, :], 0.0).astype(jnp.bfloat16)
                r = jnp.dot(d.reshape(step * ROWS, depth), rhs, preferred_element_type=jnp.float32)
                parts.append(r.reshape(step, ROWS, nz * ch))
            both = jnp.concatenate(parts, axis=1).astype(jnp.bfloat16)
            a_ref[pl.ds(l0, step), pl.ds(pl.multiple_of(i * 2 * ROWS, 2 * ROWS), 2 * ROWS), :] = both
        return carry

    lax.fori_loop(0, srcs * per // 2, associate, 0)
    zero = jnp.zeros((sub, ch), jnp.bfloat16)

    def filtering(i, carry):
        for j in range(16):
            l = i * 16 + j
            w = w_ref[l]
            rows = []
            for c0 in range(0, ch, sub):
                for z in range(nz):
                    blocks = [w[c0 : c0 + sub] if y == z else zero for y in range(nz)]
                    rows.append(jnp.concatenate(blocks, axis=1))
            r = jnp.dot(a_ref[l], jnp.concatenate(rows, axis=0), preferred_element_type=jnp.float32)
            for z in range(nz):
                t_ref[z, pl.ds(j, slots, stride=16), :] = r[:, z * ch : (z + 1) * ch]
        for z in range(nz):
            o_ref[:, :, z, pl.ds(pl.multiple_of(i * 16, 16), 16), :] = (
                t_ref[z].reshape(srcs, per * ROWS, 16, ch).astype(jnp.bfloat16)
            )
        return carry

    lax.fori_loop(0, count // 16, filtering, 0)


def mix(coeffs, tables, weights, filled, chunk, chunks, sub):
    pk, pn, src, per, rr, ln = coeffs.shape
    _, _, count, depth = tables.shape
    ch = weights.shape[1]
    nz = pn * ln // ch
    srcs = max(1, min(src, LANES // (per * ROWS)))
    slots = srcs * per * ROWS
    body = functools.partial(mix_body, slots, nz, sub, min(16, count))
    in_specs = [
        pl.BlockSpec((pk, pn, srcs, per, rr, ln), lambda i: (0, 0, i, 0, 0, 0)),
        pl.BlockSpec((srcs, per, count, depth), lambda i: (i, 0, 0, 0)),
        pl.BlockSpec((count, ch, ch), lambda i: (0, 0, 0), pipeline_mode=pl.Buffered(1)),
    ]
    args = [coeffs, tables, weights]
    alias = {}
    run = body
    if filled is not None:
        in_specs.append(pl.BlockSpec(memory_space=pl.ANY))
        args.append(filled)
        alias = {3: 0}
        run = lambda c, q, w, p, o, a, t: body(c, q, w, o, a, t)
    size = src * per * ROWS * nz * count * ch
    return pl.pallas_call(
        run,
        grid=(src // srcs,),
        in_specs=in_specs,
        out_specs=pl.BlockSpec(
            (srcs, None, per * ROWS, nz, count, ch), lambda i: (i, chunk, 0, 0, 0, 0)
        ),
        out_shape=jax.ShapeDtypeStruct((src, chunks, per * ROWS, nz, count, ch), jnp.bfloat16),
        scratch_shapes=[
            pltpu.VMEM((count, slots, nz * ch), jnp.bfloat16),
            pltpu.VMEM((nz, slots * 16, ch), jnp.float32),
        ],
        input_output_aliases=alias,
        compiler_params=pltpu.CompilerParams(vmem_limit_bytes=60 << 20),
        cost_estimate=pl.CostEstimate(
            flops=size * 2 * (depth + nz * ch),
            transcendentals=0,
            bytes_accessed=2 * (coeffs.size + tables.size + weights.size + size),
        ),
        name="mix",
    )(*args)


def body(field, conv_weight, order_map, legendre, spectral_weight):
    n_chan = lax.axis_size("chan")
    n_face = lax.axis_size("face")
    n_tile = lax.axis_size("tile")
    chan_id = lax.axis_index("chan")
    face_id = lax.axis_index("face")
    tile_id = lax.axis_index("tile")
    samples, chan_dev, cycle_dev, pix_dev = field.shape
    pixels = pix_dev * n_face
    slot_dev, cycles, degrees = legendre.shape
    owners = n_face * n_tile
    degree_dev = degrees // owners
    n_cyc = math.gcd(n_face, cycle_dev)
    n_sub = n_face // n_cyc
    cyc_own = cycle_dev // n_cyc
    sub = chan_dev // n_sub
    groups = slot_dev // ROWS
    chunks = math.gcd(4, groups)
    per = groups // chunks

    slot_start = ((chan_id * n_face + face_id) * n_tile + tile_id) * slot_dev
    own_orders = lax.dynamic_slice_in_dim(order_map, slot_start, slot_dev)
    keeping = jnp.arange(degrees, dtype=jnp.int32)[None, :] >= own_orders[:, None]
    tables = jnp.where(keeping[:, None, :], legendre, jnp.zeros_like(legendre))
    tables = tables.reshape(
        chunks, per, ROWS, n_tile, n_cyc, cyc_own, owners, degree_dev
    ).transpose(0, 6, 1, 7, 4, 3, 5, 2)
    tables = tables.reshape(chunks, owners, per, degree_dev, cycles * ROWS)

    gathered = lax.all_gather(field, "chan", axis=1, tiled=True)
    padded = extended(gathered, (("face", 3), ("tile", 2)), 1)
    padded = clear_band_edges(padded, tile_id, n_tile)
    own_weight = lax.dynamic_slice_in_dim(conv_weight, chan_id * chan_dev, chan_dev, 3)
    hidden = stencil(padded, own_weight, cycle_dev, pix_dev).astype(jnp.bfloat16)
    hidden = hidden.reshape(samples, n_sub, sub, n_cyc, cyc_own, pix_dev)
    hidden = hidden.transpose(3, 1, 4, 0, 2, 5).reshape(n_face, cyc_own, samples * sub, pix_dev)
    hidden = lax.all_to_all(hidden, "face", split_axis=0, concat_axis=0, tiled=True)
    first_cycle = tile_id * cycle_dev + (face_id // n_sub) * cyc_own
    parity = (first_cycle + jnp.arange(cyc_own, dtype=jnp.int32)) % 2
    coeffs = cycle_spectrum(hidden, parity, pixels, degrees)
    tall = pixels // LANES
    coeffs = coeffs.reshape(degrees, cyc_own * 2 * samples * sub)
    place = (order_map % tall) * (degrees // tall) + order_map // tall
    picking = (place[:, None] == jnp.arange(degrees, dtype=jnp.int32)[None, :]).astype(jnp.bfloat16)
    coeffs = jnp.dot(picking, coeffs, preferred_element_type=jnp.float32).astype(jnp.bfloat16)
    width = 2 * samples * sub
    coeffs = coeffs.reshape(n_chan, owners, chunks, per, ROWS, cyc_own, width)
    coeffs = coeffs.transpose(0, 2, 1, 3, 5, 4, 6)
    coeffs = coeffs.reshape(n_chan, chunks, owners, per, cyc_own * ROWS, width)
    coeffs = lax.all_to_all(coeffs, "chan", split_axis=0, concat_axis=0, tiled=True)

    out = None
    for chunk in range(chunks):
        got = lax.all_gather(coeffs[:, chunk], ("face", "tile"), axis=0, tiled=False)
        if n_sub > 1:
            got = got.reshape(n_cyc, n_sub, n_tile, n_chan, owners, per, cyc_own * ROWS, width)
            got = got.transpose(0, 2, 3, 4, 5, 6, 1, 7)
        got = got.reshape(n_cyc * n_tile, n_chan, owners, per, cyc_own * ROWS, n_sub * width)
        table = lax.all_to_all(
            tables[chunk], ("face", "tile"), split_axis=0, concat_axis=0, tiled=True
        )
        out = mix(got, table, spectral_weight, out, chunk, chunks, sub)
    return out.reshape(owners * slot_dev, 2, samples, degree_dev, chan_dev * n_chan)


def solution(mesh):
    in_specs = (
        P(None, "chan", "tile", "face"),
        P(),
        P(),
        P(("chan", "face", "tile"), None, None),
        P(("face", "tile"), None, None),
    )
    out_specs = P("chan", None, None, ("face", "tile"), None)
    return jax.shard_map(body, mesh=mesh, in_specs=in_specs, out_specs=out_specs, check_vma=False)
```

time: 2130 us -> 578 us (0.27)
  blocking collectives: 1460 us -> 4.58 us
  local copies, waits for them, and re-layouts: 319 us -> 63.2 us
  waiting for transfers between devices: 124 us -> 307 us
  Pallas kernels: 0 us -> 121 us
  matrix products: 112 us -> 21.6 us
  other arithmetic: 79 us -> 12 us
    all_to_all x2 -> x1, blocking collectives: 1460 us -> 4.58 us  [body(): lax.all_to_all(coeffs, 'chan', split_axis=0, concat_axis=0, tiled=True)]
    all_to_all x1 -> x5, waiting for transfers between devices: 25.8 us -> 199 us  [the longest x4 186 us: body(): lax.all_to_all(tables[chunk], ('face', 'tile'), split_axis=0, concat_axis...]
    reshape x3 -> x1, local copies, waits for them, and re-layouts: 162 us -> 3.38 us  [body(): coeffs = coeffs.reshape(degrees, cyc_own * 2 * samples * sub)]
    pallas_call x0 -> x4, Pallas kernels: none -> 121 us  [mix(): pl.pallas_call(run, grid=(src // srcs,), in_specs=in_specs, out_specs=pl....]
    dot_general x6 -> x3, matrix products: 105 us -> 12.9 us  [the longest x1 7.87 us: cycle_spectrum(): jnp.einsum('imrxb,izrbk->mkrzx', turned, second, precision=lax.Precision....]
    reduce_scatter x1 -> x0, waiting for transfers between devices: 84.7 us -> none  [body(): lax.psum_scatter(jnp.stack(halves, axis=-1).reshape(lax.axis_size('face')...]
    cos x1 -> x2, other arithmetic: 71.9 us -> 0.3 us  [unit(): return (jnp.cos(angle), -jnp.sin(angle))]
    all_gather x0 -> x4, waiting for transfers between devices: none -> 69.7 us  [body(): lax.all_gather(coeffs[:, chunk], ('face', 'tile'), axis=0, tiled=False)]
  transfers between devices with their start and end apart: 7 -> 14, of which waited for: 5 -> 11; matrix products, arithmetic and copies ran while one was open for 4% -> 9% of each run, Pallas kernels for 0% -> 16%
where the time goes in v1:
time: 578 us; the launch traced here: 570 us
  waiting for transfers between devices  307 us (53%)
  Pallas kernels  121 us (21%)
  local copies, waits for them, and re-layouts  63.2 us (11%)
  starting transfers between devices  27.6 us (5%)
  matrix products  21.6 us (4%)
  between operations  13.8 us (2%)
  other arithmetic  12 us (2%)
    all_to_all x4, waiting for transfers between devices, body(): lax.all_to_all(tables[chunk], ('face', 'tile'), split_axis=0, concat_axis...  186 us
    pallas_call x4, Pallas kernels, mix(): pl.pallas_call(run, grid=(src // srcs,), in_specs=in_specs, out_specs=pl....  121 us
    all_gather x4, waiting for transfers between devices, body(): lax.all_gather(coeffs[:, chunk], ('face', 'tile'), axis=0, tiled=False)  69.7 us
    slice x5, local copies, waits for them, and re-layouts, body(): tables[chunk]  19.1 us
    all_to_all x4, starting transfers between devices, body(): lax.all_to_all(tables[chunk], ('face', 'tile'), split_axis=0, concat_axis...  16.6 us
    unnamed x15, local copies, waits for them, and re-layouts  15.7 us
    all_gather x1, waiting for transfers between devices, body(): gathered = lax.all_gather(field, 'chan', axis=1, tiled=True)  13.3 us
    ppermute x2, waiting for transfers between devices, extended(): before = lax.ppermute(last, axis, up)  13.3 us
  transfers between devices with their start and end apart: 14, of which 11 were waited for; matrix products, arithmetic and copies ran while one was open for 9% of the time, Pallas kernels for 16%

profile of v1, /device:TPU:0, one launch (start us, length us, event | category | flops | bytes accessed | tf_op | source)
XLA Modules:
  0.0 569.9 jit_solution(2732159594902797198)
XLA Ops:
  6.5 2.8 copy.47
  9.5 13.3 %all-gather.10.cloned.1.call-done = bf16[1,128,8,1024]{3,1,2,0:T(8,128)(2,1)} async-done(((bf16[1,64,8,1024]{3,1,2,0:T(8,128)(2,1)}), bf16[1,128,8,1024]{3,1,2,0:T(8,128)(2,1)}) %all-gather.10.cloned.1.call-update) | async-done | bytes 2097168 | tf_op jit(solution)/shard_map/all_gather | solution.py:202
  22.8 1.2 fusion.63
  24.0 1.8 collective-permute-start
  25.8 1.2 collective-permute-start.1
  27.9 6.2 %collective-permute-done = bf16[1,128,8,1]{3,1,2,0:T(8,128)(2,1)S(1)} collective-permute-done((bf16[1,128,8,1]{3,1,2,0:T(8,128)(2,1)S(1)}, bf16[1,128,8,1]{3,1,2,0:T(8,128)(2,1)S(1)}, u32[]{:S(2)}, u32[]{:S(2)}) %collective-permute-start) | collective-permute-done | bytes 2080 | tf_op jit(solution)/shard_map/ppermute | solution.py:22
  34.1 5.2 collective-permute-done.1
  39.4 4.8 concatenate.15
  45.1 1.5 collective-permute-start.2
  46.6 2.3 collective-permute-start.3
  49.9 7.1 %collective-permute-done.2 = bf16[1,128,1,1026]{3,1,2,0:T(8,128)(2,1)S(1)} collective-permute-done((bf16[1,128,1,1026]{3,1,2,0:T(8,128)(2,1)}, bf16[1,128,1,1026]{3,1,2,0:T(8,128)(2,1)S(1)}, u32[]{:S(2)}, u32[]{:S(2)}) %collective-permute-start.2) | collective-permute-done | bytes 262688 | tf_op jit(solution)/shard_map/ppermute | solution.py:22
  57.0 4.2 collective-permute-done.3
  67.9 2.5 add_convert_fusion
  70.4 3.6 all-to-all-start
  74.7 12.9 %all-to-all-done = bf16[4,2,64,1024]{3,2,1,0:T(8,128)(2,1)S(1)} async-done(((bf16[4,2,64,1024]{3,2,1,0:T(8,128)(2,1)}), bf16[4,2,64,1024]{3,2,1,0:T(8,128)(2,1)S(1)}, u32[]{:S(2)}, u32[]{:S(2)}) %all-to-all-start) | async-done | bytes 1048608 | tf_op jit(solution)/shard_map/all_to_all | solution.py:209
  87.8 1.8 convolution_bitcast_fusion
  91.0 7.9 %fusion.5 = bf16[32,64,2,2,64]{4,1,0,3,2:T(8,128)(2,1)S(1)} fusion(f32[2,32,2,64,128,1]{4,1,3,2,0,5:T(8,128)S(1)} %maximum_bitcast_fusion, f32[1,2,2,128,64]{3,4,0,1,2:T(8,128)S(1)} %get-tuple-element.20, f32[1,2,2,128,64]{3,4,0,1,2:T(8,128)S(1)} %get-tuple-element.19), kind=kOutput, calls=%fused_computation.11 | convolution fusion | flops 1611202560 | bytes 5505024 | tf_op jit(solution)/shard_map/imrxb,izrbk->mkrzx/dot_general | solution.py:73
  98.9 3.8 copy.50
  102.7 3.4 reshape.415
  106.1 3.2 fusion.4
  109.5 4.6 all_to_all.30
  114.0 1.0 fusion.64
  116.1 7.6 %broadcast_select_fusion = bf16[64,32,2048]{2,1,0:T(8,128)(2,1)} fusion(bf16[64,32,2048]{2,1,0:T(8,128)(2,1)} %param.8, pred[64,2048]{1,0:T(8,128)(4,1)S(1)} %iota_compare_fusion.4), kind=kLoop, calls=%fused_computation.3 | loop fusion | flops 4194304 | bytes 16908288 | tf_op jit(solution)/shard_map/jit(_where)/select_n | solution.py:196
  123.7 9.8 %copy.80 = bf16[256,8,16,128]{3,2,1,0:T(8,128)(2,1)} copy(bf16[256,8,16,128]{3,1,2,0:T(8,128)(2,1)} %bitcast.155) | data formatting | bytes 16777216
  133.5 6.2 %fusion.61 = (bf16[1,16,2,128,4,4,2,8]{3,1,6,4,5,7,2,0:T(8,128)(2,1)S(1)}, bf16[1,16,2,128,4,4,2,8]{3,1,6,4,5,7,2,0:T(8,128)(2,1)}, bf16[1,16,2,128,4,4,2,8]{3,1...) fusion(bf16[4,16,2,128,4,4,2,8]{3,1,6,4,5,7,2,0:T(8,128)(2,1)} %bitcast.154), kind=kLoop, calls=%fused_computation.119 | loop fusion | bytes 16777216 | tf_op jit(solution)/shard_map/slice | solution.py:232
  139.7 1.4 copy.58
  141.0 2.6 copy.59
  143.7 4.0 all-to-all-start.5
  148.3 4.3 copy.56
  152.7 3.9 copy.57
  156.6 68.7 %all-to-all-done.5.q_ref = bf16[16,2,128,256]{3,2,1,0:T(8,128)(2,1)S(1)} async-done(((bf16[16,2,128,256]{3,2,1,0:T(8,128)(2,1)}), bf16[16,2,128,256]{3,2,1,0:T(8,128)(2,1)S(1)}, u32[]{:S(2)}, u32[]{:S(2)}) %all-to-all-start.5) | async-done | bytes 2097184 | tf_op jit(solution)/shard_map/all_to_all | solution.py:231
  225.3 1.4 copy-done.4
  226.7 3.7 all-to-all-start.4
  230.4 4.3 copy.54
  234.6 3.9 copy.55
  238.6 58.5 %all-to-all-done.4.q = bf16[16,2,128,256]{3,2,1,0:T(8,128)(2,1)S(1)} async-done(((bf16[16,2,128,256]{3,2,1,0:T(8,128)(2,1)}), bf16[16,2,128,256]{3,2,1,0:T(8,128)(2,1)S(1)}, u32[]{:S(2)}, u32[]{:S(2)}) %all-to-all-start.4) | async-done | bytes 2097184 | tf_op jit(solution)/shard_map/all_to_all | solution.py:231
  297.1 1.4 copy-done.2
  298.5 4.4 all-to-all-start.3
  303.5 3.0 copy.52
  306.5 2.6 copy.53
  309.1 59.2 %all-to-all-done.3.q = bf16[16,2,128,256]{3,2,1,0:T(8,128)(2,1)} async-done(((bf16[16,2,128,256]{3,2,1,0:T(8,128)(2,1)}), bf16[16,2,128,256]{3,2,1,0:T(8,128)(2,1)}, u32[]{:S(2)}, u32[]{:S(2)}) %all-to-all-start.3) | async-done | bytes 2097184 | tf_op jit(solution)/shard_map/all_to_all | solution.py:231
  368.3 4.4 all-to-all-start.2
  372.7 30.1 %mix.4.p = bf16[16,4,16,2,128,128]{5,4,3,2,1,0:T(8,128)(2,1)} custom-call(bf16[16,2,16,2,16,128]{5,4,3,2,1,0:T(8,128)(2,1)} %bitcast.160, bf16[16,2,128,256]{3,2,1,0:T(8,128)(2,1)} %copy-done.4, bf16[128,128,128]{2,1,0:T(8,128)(2,1)} %w.5), custom_call_target="tpu_custom_call" | custom-call | flops 8589934592 | bytes 27262976 | tf_op jit(solution)/shard_map/mix/pallas_call | solution.py:150
  402.9 30.1 %mix.5.p = bf16[16,4,16,2,128,128]{5,4,3,2,1,0:T(8,128)(2,1)} custom-call(bf16[16,2,16,2,16,128]{5,4,3,2,1,0:T(8,128)(2,1)} %bitcast.161, bf16[16,2,128,256]{3,2,1,0:T(8,128)(2,1)} %copy-done.2, bf16[128,128,128]{2,1,0:T(8,128)(2,1)} %w.5, bf16[16,4,16,2,128,128]{5,4,3,2,1,0:T(8,128)(2,1)} %mix.4.p), custom_call_target="tpu_custom_call", output_to_operand_aliasing={{}: (3, {})} | custom-call | flops 8589934592 | bytes 27262976 | tf_op jit(solution)/shard_map/mix/pallas_call | solution.py:150
  433.0 22.8 %all-gather.14.cloned.1.call-done = bf16[32,1,16,2,16,128]{5,4,3,2,1,0:T(8,128)(2,1)} async-done(((bf16[2,1,16,2,16,128]{5,4,3,2,1,0:T(8,128)(2,1)}), bf16[32,1,16,2,16,128]{5,4,3,2,1,0:T(8,128)(2,1)}) %all-gather.14.cloned.1.call-update) | async-done | bytes 4194320 | tf_op jit(solution)/shard_map/all_gather | solution.py:226
  455.8 30.1 %mix.6.p = bf16[16,4,16,2,128,128]{5,4,3,2,1,0:T(8,128)(2,1)} custom-call(bf16[16,2,16,2,16,128]{5,4,3,2,1,0:T(8,128)(2,1)} %bitcast.162, bf16[16,2,128,256]{3,2,1,0:T(8,128)(2,1)} %all-to-all-done.3.q, bf16[128,128,128]{2,1,0:T(8,128)(2,1)} %w.5, bf16[16,4,16,2,128,128]{5,4,3,2,1,0:T(8,128)(2,1)} %mix.5.p), custom_call_target="tpu_custom_call", output_to_operand_aliasing={{}: (3, {})} | custom-call | flops 8589934592 | bytes 27262976 | tf_op jit(solution)/shard_map/mix/pallas_call | solution.py:150
  485.9 46.9 %all-gather.12.cloned.1.call-done = bf16[32,1,16,2,16,128]{5,4,3,2,1,0:T(8,128)(2,1)} async-done(((bf16[2,1,16,2,16,128]{5,4,3,2,1,0:T(8,128)(2,1)}), bf16[32,1,16,2,16,128]{5,4,3,2,1,0:T(8,128)(2,1)}) %all-gather.12.cloned.1.call-update) | async-done | bytes 4194320 | tf_op jit(solution)/shard_map/all_gather | solution.py:226
  532.8 30.2 %mix.7 = bf16[16,4,16,2,128,128]{5,4,3,2,1,0:T(8,128)(2,1)} custom-call(bf16[16,2,16,2,16,128]{5,4,3,2,1,0:T(8,128)(2,1)} %bitcast.163, bf16[16,2,128,256]{3,2,1,0:T(8,128)(2,1)} %copy-done.3, bf16[128,128,128]{2,1,0:T(8,128)(2,1)} %w.5, bf16[16,4,16,2,128,128]{5,4,3,2,1,0:T(8,128)(2,1)} %mix.6.p), custom_call_target="tpu_custom_call", output_to_operand_aliasing={{}: (3, {})} | custom-call | flops 8589934592 | bytes 27262976 | tf_op jit(solution)/shard_map/mix/pallas_call | solution.py:150
  (50 shorter events, 14.0 us)
Async XLA Ops:
  6.5 55.2 %copy-start = (bf16[3,3,128,128]{3,2,1,0:T(8,128)(2,1)S(1)}, bf16[3,3,128,128]{3,2,1,0:T(8,128)(2,1)}, u32[]{:S(2)}) copy-start(bf16[3,3,128,128]{3,2,1,0:T(8,128)(2,1)} %param.6) | copy-start | bytes 884740
  6.5 16.3 %all-gather.10.cloned.1.call-start = ((), (), s32[]{:S(2)}) async-start(), calls=%async_computation.6 | async-start | bytes 3145728 | tf_op jit(solution)/shard_map/all_gather | solution.py:202
  24.0 10.1 %collective-permute-start = (bf16[1,128,8,1]{3,1,2,0:T(8,128)(2,1)S(1)}, bf16[1,128,8,1]{3,1,2,0:T(8,128)(2,1)S(1)}, u32[]{:S(2)}, u32[]{:S(2)}) collective-permute-start(bf16[1,128,8,1]{3,1,2,0:T(8,128)(2,1)S(1)} %get-tuple-element.14), channel_id=1, source_target_pairs={{0,4},{4,8},{8,12},{12,0},{1,5},{5,9},{9,13},{13,1},{2,6},{6,10},{... | collective-permute-start | bytes 6152 | tf_op jit(solution)/shard_map/ppermute | solution.py:22
  25.8 13.6 %collective-permute-start.1 = (bf16[1,128,8,1]{3,1,2,0:T(8,128)(2,1)S(1)}, bf16[1,128,8,1]{3,1,2,0:T(8,128)(2,1)S(1)}, u32[]{:S(2)}, u32[]{:S(2)}) collective-permute-start(bf16[1,128,8,1]{3,1,2,0:T(8,128)(2,1)S(1)} %get-tuple-element.13), channel_id=1, source_target_pairs={{4,0},{8,4},{12,8},{0,12},{5,1},{9,5},{13,9},{1,13},{6,2},{10,6},{... | collective-permute-start | bytes 6152 | tf_op jit(solution)/shard_map/ppermute | solution.py:23
  45.1 11.9 %collective-permute-start.2 = (bf16[1,128,1,1026]{3,1,2,0:T(8,128)(2,1)}, bf16[1,128,1,1026]{3,1,2,0:T(8,128)(2,1)S(1)}, u32[]{:S(2)}, u32[]{:S(2)}) collective-permute-start(bf16[1,128,1,1026]{3,1,2,0:T(8,128)(2,1)} %get-tuple-element.11), channel_id=1, source_target_pairs={{0,1},{1,2},{2,3},{3,0},{4,5},{5,6},{6,7},{7,4},{8,9},{9,10},{10,1... | collective-permute-start | bytes 787976 | tf_op jit(solution)/shard_map/ppermute | solution.py:22
  46.6 14.6 %collective-permute-start.3 = (bf16[1,128,1,1026]{3,1,2,0:T(8,128)(2,1)}, bf16[1,128,1,1026]{3,1,2,0:T(8,128)(2,1)S(1)}, u32[]{:S(2)}, u32[]{:S(2)}) collective-permute-start(bf16[1,128,1,1026]{3,1,2,0:T(8,128)(2,1)} %get-tuple-element.12), channel_id=1, source_target_pairs={{1,0},{2,1},{3,2},{0,3},{5,4},{6,5},{7,6},{4,7},{9,8},{10,9},{11,1... | collective-permute-start | bytes 787976 | tf_op jit(solution)/shard_map/ppermute | solution.py:23
  70.4 3.9 copy-start.5
  70.4 17.1 %all-to-all-start = ((bf16[4,2,64,1024]{3,2,1,0:T(8,128)(2,1)}), bf16[4,2,64,1024]{3,2,1,0:T(8,128)(2,1)S(1)}, u32[]{:S(2)}, u32[]{:S(2)}) async-start(bf16[4,2,64,1024]{3,2,1,0:T(8,128)(2,1)} %bitcast.36), calls=%async_computation | async-start | bytes 2097152 | tf_op jit(solution)/shard_map/all_to_all | solution.py:209
  74.1 298.6 %all-gather.18.cloned.1.call-start = ((), (), s32[]{:S(2)}) async-start(), calls=%async_computation.10 | async-start | bytes 4456448 | tf_op jit(solution)/shard_map/all_gather | solution.py:226
  115.1 287.8 %all-gather.16.cloned.1.call-start = ((), (), s32[]{:S(2)}) async-start(), calls=%async_computation.9 | async-start | bytes 4456448 | tf_op jit(solution)/shard_map/all_gather | solution.py:226
  143.7 81.6 %all-to-all-start.5 = ((bf16[16,2,128,256]{3,2,1,0:T(8,128)(2,1)}), bf16[16,2,128,256]{3,2,1,0:T(8,128)(2,1)S(1)}, u32[]{:S(2)}, u32[]{:S(2)}) async-start(bf16[16,2,128,256]{3,2,1,0:T(8,128)(2,1)} %copy.59), calls=%async_computation.5 | async-start | bytes 4194304 | tf_op jit(solution)/shard_map/all_to_all | solution.py:231
  147.7 308.0 %all-gather.14.cloned.1.call-start = ((), (), s32[]{:S(2)}) async-start(), calls=%async_computation.8 | async-start | bytes 4456448 | tf_op jit(solution)/shard_map/all_gather | solution.py:226
  225.3 1.4 copy-start.4
  226.7 70.4 %all-to-all-start.4 = ((bf16[16,2,128,256]{3,2,1,0:T(8,128)(2,1)}), bf16[16,2,128,256]{3,2,1,0:T(8,128)(2,1)S(1)}, u32[]{:S(2)}, u32[]{:S(2)}) async-start(bf16[16,2,128,256]{3,2,1,0:T(8,128)(2,1)} %copy.57), calls=%async_computation.4 | async-start | bytes 4194304 | tf_op jit(solution)/shard_map/all_to_all | solution.py:231
  297.1 1.4 copy-start.2
  298.5 69.8 %all-to-all-start.3 = ((bf16[16,2,128,256]{3,2,1,0:T(8,128)(2,1)}), bf16[16,2,128,256]{3,2,1,0:T(8,128)(2,1)}, u32[]{:S(2)}, u32[]{:S(2)}) async-start(bf16[16,2,128,256]{3,2,1,0:T(8,128)(2,1)} %copy.55), calls=%async_computation.3 | async-start | bytes 4194304 | tf_op jit(solution)/shard_map/all_to_all | solution.py:231
  302.9 229.8 %all-gather.12.cloned.1.call-start = ((), (), s32[]{:S(2)}) async-start(), calls=%async_computation.7 | async-start | bytes 4456448 | tf_op jit(solution)/shard_map/all_gather | solution.py:226
  368.3 117.6 %all-to-all-start.2 = ((bf16[16,2,128,256]{3,2,1,0:T(8,128)(2,1)}), bf16[16,2,128,256]{3,2,1,0:T(8,128)(2,1)S(1)}, u32[]{:S(2)}, u32[]{:S(2)}) async-start(bf16[16,2,128,256]{3,2,1,0:T(8,128)(2,1)} %copy.53), calls=%async_computation.2 | async-start | bytes 4194304 | tf_op jit(solution)/shard_map/all_to_all | solution.py:231
  485.9 46.9 %copy-start.3 = (bf16[16,2,128,256]{3,2,1,0:T(8,128)(2,1)}, bf16[16,2,128,256]{3,2,1,0:T(8,128)(2,1)S(1)}, u32[]{:S(2)}) copy-start(bf16[16,2,128,256]{3,2,1,0:T(8,128)(2,1)S(1)} %all-to-all-done.2.q) | copy-start | bytes 6291460
  532.8 30.2 %copy-start.1 = (bf16[3,3,128,128]{3,2,1,0:T(8,128)(2,1)S(1)}, bf16[3,3,128,128]{3,2,1,0:T(8,128)(2,1)}, u32[]{:S(2)}) copy-start(bf16[3,3,128,128]{3,2,1,0:T(8,128)(2,1)} %param.6) | copy-start | bytes 884740
Sparse Core Ops, SparseCore 0:
  9.5 13.2 all-gather.9
  115.2 103.7 all-gather.17
  221.8 131.0 all-gather.15
  355.5 100.2 all-gather.13
  458.4 74.3 all-gather.11

commit v2 on v1

v2 whole, which is shorter than its diff:
```python
import functools
import math

import jax
import jax.numpy as jnp
import numpy as np
from jax import lax
from jax.experimental import pallas as pl
from jax.experimental.pallas import tpu as pltpu
from jax.sharding import PartitionSpec as P


LANES = 128
ROWS = 8
STRIDE = 17


def extended(field):
    n_face, n_tile = lax.axis_size("face"), lax.axis_size("tile")
    above = lax.ppermute(field[:, :, -1], "tile", [(i, i + 1) for i in range(n_tile - 1)])
    below = lax.ppermute(field[:, :, 0], "tile", [(i + 1, i) for i in range(n_tile - 1)])
    above, below = above[:, :, None], below[:, :, None]
    sides = []
    for pixel, step in ((-1, 1), (0, n_face - 1)):
        column = jnp.concatenate(
            [x[:, :, :, pixel] for x in (above, field, below)], axis=2
        ).transpose(0, 2, 1)
        pairs = [(i, (i + step) % n_face) for i in range(n_face)]
        column = lax.ppermute(column, "face", pairs)
        sides.append(column.transpose(0, 2, 1)[:, :, :, None])
    whole = jnp.concatenate([above, field, below], axis=2)
    return jnp.concatenate([sides[0], whole, sides[1]], axis=3)


def stencil(padded, weights, cycle_count, pix_count):
    summed = None
    for shift_r in range(3):
        for shift_p in range(3):
            window = padded[:, :, shift_r : shift_r + cycle_count, shift_p : shift_p + pix_count]
            contrib = jnp.einsum(
                "birp,io->borp",
                window,
                weights[shift_r, shift_p],
                preferred_element_type=jnp.float32,
            )
            summed = contrib if summed is None else summed + contrib
    return summed


def unit(turns, period):
    angle = (turns % (2 * period)).astype(jnp.float32) * (math.pi / period)
    return jnp.cos(angle), -jnp.sin(angle)


def cycle_spectrum(rows, pieces, parity, pixels, orders):
    parts, n_r, n_x, pix = rows.shape
    count = pixels // LANES
    tops = orders // count
    a = pieces[:, None] * (pix // LANES) + jnp.arange(pix // LANES, dtype=jnp.int32)[None, :]
    a = a.reshape(count)
    m1 = jnp.arange(count, dtype=jnp.int32)
    k = jnp.arange(tops, dtype=jnp.int32)
    half = 2 * jnp.arange(LANES, dtype=jnp.int32)[None, :] + parity[:, None]
    first = jnp.stack(unit(2 * m1[:, None] * a[None, :], count))
    first = first.reshape(2, count, parts, pix // LANES)
    x = rows.reshape(parts, n_r, n_x, pix // LANES, LANES).astype(jnp.float32)
    y = jnp.einsum("zmfa,frxab->zmrxb", first, x, precision=lax.Precision.HIGHEST)
    tw_re, tw_im = unit(m1[:, None, None] * half[None], pixels)
    tw_re, tw_im = tw_re[:, :, None], tw_im[:, :, None]
    turned = jnp.stack([y[0] * tw_re - y[1] * tw_im, y[0] * tw_im + y[1] * tw_re])
    g_re, g_im = unit(half[:, :, None] * k[None, None, :], LANES)
    second = jnp.stack([jnp.stack([g_re, g_im]), jnp.stack([-g_im, g_re])])
    return jnp.einsum(
        "imrxb,izrbk->rzmkx", turned, second, precision=lax.Precision.HIGHEST
    ).astype(jnp.bfloat16)


def table_body(n_tile, n_cyc, cyc_own, late, leg_ref, order_ref, *out_refs):
    _, count, depth = out_refs[0].shape
    cycles = depth // ROWS
    dest = pl.program_id(0)
    lanes = lax.broadcasted_iota(jnp.int32, (1, depth), 1)
    slot, rest = lanes % ROWS, lanes // ROWS
    cyc, rest = rest % cyc_own, rest // cyc_own
    rows = lax.broadcasted_iota(jnp.int32, (depth, depth), 0)

    def moving(back, part):
        tile = (dest % n_tile - back + n_tile) % n_tile
        source = slot * cycles + (tile * n_cyc + part) * cyc_own + cyc
        return jnp.where(rows == source, 1.0, 0.0).astype(jnp.bfloat16)

    usual = moving(rest % n_tile, rest // n_tile)
    other = moving(rest // n_cyc, rest % n_cyc)
    degree = dest * count + lax.broadcasted_iota(jnp.int32, (count, depth), 0)
    places = [(ref, i) for ref in out_refs for i in range(ref.shape[0])]
    for g, (ref, i) in enumerate(places):
        x = leg_ref[g * ROWS : (g + 1) * ROWS].reshape(depth, count)
        y = lax.dot_general(
            x,
            usual if g < late else other,
            (((0,), (0,)), ((), ())),
            preferred_element_type=jnp.float32,
        )
        ref[i] = jnp.where(degree >= order_ref[g], y, 0.0).astype(jnp.bfloat16)


def tables_for(legendre, orders, sizes, late, owners, n_tile, n_cyc, cyc_own):
    slots, cycles, degrees = legendre.shape
    count = degrees // owners
    groups = slots // ROWS
    depth = cycles * ROWS
    lane_orders = jnp.tile(orders.reshape(groups, 1, ROWS), (1, 1, cycles))
    return pl.pallas_call(
        functools.partial(table_body, n_tile, n_cyc, cyc_own, late),
        grid=(owners,),
        in_specs=[
            pl.BlockSpec((slots, cycles, count), lambda d: (0, 0, d)),
            pl.BlockSpec((groups, 1, depth), lambda d: (0, 0, 0)),
        ],
        out_specs=[
            pl.BlockSpec((None, n, count, depth), lambda d: (d, 0, 0, 0)) for n in sizes
        ],
        out_shape=[jax.ShapeDtypeStruct((owners, n, count, depth), jnp.bfloat16) for n in sizes],
        compiler_params=pltpu.CompilerParams(vmem_limit_bytes=24 << 20),
        cost_estimate=pl.CostEstimate(
            flops=2 * owners * groups * count * depth * depth,
            transcendentals=0,
            bytes_accessed=4 * owners * groups * count * depth,
        ),
        name="tables",
    )(legendre, lane_orders)


def plain_tables(legendre, orders, n_face, n_tile, n_cyc, cyc_own):
    slots, cycles, degrees = legendre.shape
    owners = n_face * n_tile
    per = slots // ROWS
    keeping = jnp.arange(degrees, dtype=jnp.int32)[None, :] >= orders[:, None]
    tables = jnp.where(keeping[:, None, :], legendre, jnp.zeros_like(legendre))
    tables = tables.reshape(
        per, ROWS, n_tile, n_cyc, cyc_own, n_face, n_tile, degrees // owners
    )
    turned = []
    for t in range(n_tile):
        back = [(t - k) % n_tile for k in range(n_tile)]
        turned.append(tables[:, :, jnp.array(back), :, :, :, t])
    tables = jnp.stack(turned, axis=6)
    tables = tables.transpose(5, 6, 0, 7, 3, 2, 4, 1)
    return tables.reshape(owners, per, degrees // owners, cycles * ROWS)


def partner(index, k, count):
    return index ^ k if count & (count - 1) == 0 else (k - index) % count


def swapped(blocks, axis):
    count = lax.axis_size(axis)
    index = lax.axis_index(axis)
    found = []
    for k in range(count):
        pairs = [(i, partner(i, k, count)) for i in range(count)]
        block = lax.dynamic_index_in_dim(blocks, partner(index, k, count), 0, keepdims=False)
        moves = any(i != j for i, j in pairs)
        found.append(lax.ppermute(block, axis, pairs) if moves else block)
    return jnp.stack(found)


def along_tiles(piece):
    n_tile = lax.axis_size("tile")
    tile_id = lax.axis_index("tile")
    up = [(i, i + 1) for i in range(n_tile - 1)]
    down = [(i + 1, i) for i in range(n_tile - 1)]
    rising, falling = [piece], [piece]
    for _ in range(n_tile - 1):
        rising.append(lax.ppermute(rising[-1], "tile", up))
        falling.append(lax.ppermute(falling[-1], "tile", down))
    parts = [piece]
    for k in range(1, n_tile):
        parts.append(jnp.where(tile_id >= k, rising[k], falling[n_tile - k]))
    return jnp.stack(parts)


def mix_body(slots, nz, sub, step, c_ref, w_ref, *refs):
    *q_refs, o_ref, a_ref, t_ref = refs
    pk, pn, srcs, per, rr, ln = c_ref.shape
    depth = pk * rr
    count, ch = w_ref.shape[0], w_ref.shape[1]
    lane = lax.broadcasted_iota(jnp.int32, (1, ROWS, depth), 2)
    row = lax.broadcasted_iota(jnp.int32, (1, ROWS, depth), 1)
    own = (lane % ROWS) == row

    def associate(i, carry):
        held = []
        for h in range(2):
            a, b = (i, h) if per == 2 else ((2 * i + h) // per, (2 * i + h) % per)
            rhs = [c_ref[:, n, a, b].reshape(depth, ln) for n in range(pn)]
            held.append((a, b, jnp.concatenate(rhs, axis=1)))
        for l0 in range(0, count, step):
            parts = []
            for a, b, rhs in held:
                q_ref, at = (q_refs[0], b) if len(q_refs) == 1 else (q_refs[b], 0)
                q = q_ref[a, at, pl.ds(l0, step), :].astype(jnp.float32)
                d = jnp.where(own, q[:, None, :], 0.0).astype(jnp.bfloat16)
                r = jnp.dot(d.reshape(step * ROWS, depth), rhs, preferred_element_type=jnp.float32)
                parts.append(r.reshape(step, ROWS, nz * ch))
            both = jnp.concatenate(parts, axis=1).astype(jnp.bfloat16)
            a_ref[pl.ds(l0, step), pl.ds(pl.multiple_of(i * 2 * ROWS, 2 * ROWS), 2 * ROWS), :] = both
        return carry

    lax.fori_loop(0, srcs * per // 2, associate, 0)
    zero = jnp.zeros((sub, ch), jnp.bfloat16)

    def filtering(i, carry):
        for j in range(16):
            l = i * 16 + j
            w = w_ref[l]
            rows = []
            for c0 in range(0, ch, sub):
                for z in range(nz):
                    blocks = [w[c0 : c0 + sub] if y == z else zero for y in range(nz)]
                    rows.append(jnp.concatenate(blocks, axis=1))
            r = jnp.dot(a_ref[l], jnp.concatenate(rows, axis=0), preferred_element_type=jnp.float32)
            for z in range(nz):
                t_ref[z, pl.ds(j, slots, stride=STRIDE), :] = r[:, z * ch : (z + 1) * ch]
        at = pl.ds(pl.multiple_of(i * 16, 16), 16)
        for z in range(nz):
            for x in range(slots):
                o_ref[x // (per * ROWS), x % (per * ROWS), z, at, :] = t_ref[
                    z, pl.ds(x * STRIDE, 16), :
                ].astype(jnp.bfloat16)
        return carry

    lax.fori_loop(0, count // 16, filtering, 0)


def mix(coeffs, tables, weights, filled, chunk, chunks, sub):
    pk, pn, src, per, rr, ln = coeffs.shape
    count, depth = tables[0].shape[2:]
    ch = weights.shape[1]
    nz = pn * ln // ch
    srcs = max(1, min(src, LANES // (per * ROWS)))
    slots = srcs * per * ROWS
    body = functools.partial(mix_body, slots, nz, sub, min(16, count))
    in_specs = [
        pl.BlockSpec((pk, pn, srcs, per, rr, ln), lambda i: (0, 0, i, 0, 0, 0)),
        pl.BlockSpec((count, ch, ch), lambda i: (0, 0, 0), pipeline_mode=pl.Buffered(1)),
    ]
    for table in tables:
        in_specs.append(pl.BlockSpec((srcs, table.shape[1], count, depth), lambda i: (i, 0, 0, 0)))
    args = [coeffs, weights, *tables]
    alias = {}
    run = body
    if filled is not None:
        alias = {len(args): 0}
        in_specs.append(pl.BlockSpec(memory_space=pl.ANY))
        args.append(filled)
        run = lambda *refs: body(*refs[: len(args) - 1], *refs[len(args) :])
    size = src * per * ROWS * nz * count * ch
    return pl.pallas_call(
        run,
        grid=(src // srcs,),
        in_specs=in_specs,
        out_specs=pl.BlockSpec(
            (srcs, None, per * ROWS, nz, count, ch), lambda i: (i, chunk, 0, 0, 0, 0)
        ),
        out_shape=jax.ShapeDtypeStruct((src, chunks, per * ROWS, nz, count, ch), jnp.bfloat16),
        scratch_shapes=[
            pltpu.VMEM((count, slots, nz * ch), jnp.bfloat16),
            pltpu.VMEM((nz, slots * STRIDE, ch), jnp.float32),
        ],
        input_output_aliases=alias,
        compiler_params=pltpu.CompilerParams(vmem_limit_bytes=60 << 20),
        cost_estimate=pl.CostEstimate(
            flops=size * 2 * (depth + nz * ch),
            transcendentals=0,
            bytes_accessed=2 * (coeffs.size + sum(t.size for t in tables) + weights.size + size),
        ),
        name="mix",
    )(*args)


def body(field, conv_weight, order_map, legendre, spectral_weight):
    n_chan = lax.axis_size("chan")
    n_face = lax.axis_size("face")
    n_tile = lax.axis_size("tile")
    chan_id = lax.axis_index("chan")
    face_id = lax.axis_index("face")
    tile_id = lax.axis_index("tile")
    samples, chan_dev, cycle_dev, pix_dev = field.shape
    pixels = pix_dev * n_face
    slot_dev, _, degrees = legendre.shape
    owners = n_face * n_tile
    degree_dev = degrees // owners
    n_cyc = math.gcd(n_face, cycle_dev)
    n_sub = n_face // n_cyc
    cyc_own = cycle_dev // n_cyc
    sub = chan_dev // n_sub
    groups = slot_dev // ROWS
    per = math.gcd(2, groups)
    chunks = groups // per
    sizes = [[1] * per if c == 1 else [per] for c in range(chunks)]
    late = chunks - 1 if chunks > 2 and n_sub == 1 and degree_dev >= LANES else chunks

    slot_start = ((chan_id * n_face + face_id) * n_tile + tile_id) * slot_dev
    own_orders = lax.dynamic_slice_in_dim(order_map, slot_start, slot_dev)
    if degree_dev >= LANES:
        tables = tables_for(legendre, own_orders, sum(sizes, []), late * per, owners, n_tile, n_cyc, cyc_own)
    else:
        tables = plain_tables(legendre, own_orders, n_face, n_tile, n_cyc, cyc_own)
        tables = jnp.split(tables, list(np.cumsum(sum(sizes, []))[:-1]), axis=1)
    weights = jnp.roll(spectral_weight, -chan_id * chan_dev, axis=1)

    padded = extended(field)
    padded = lax.all_gather(padded, "chan", axis=1, tiled=True)

    fetched = []
    tables = list(tables)
    for c in range(chunks):
        parts = []
        for _ in range(len(sizes[c])):
            parts.append(
                lax.all_to_all(
                    tables.pop(0), ("face", "tile"), split_axis=0, concat_axis=0, tiled=True
                )
            )
        fetched.append(parts)
    own_weight = lax.dynamic_slice_in_dim(conv_weight, chan_id * chan_dev, chan_dev, 3)
    hidden = stencil(padded, own_weight, cycle_dev, pix_dev).astype(jnp.bfloat16)
    hidden = hidden.reshape(samples, n_sub, sub, n_cyc, cyc_own, pix_dev)
    hidden = hidden.transpose(3, 1, 4, 0, 2, 5).reshape(n_face, cyc_own, samples * sub, pix_dev)
    hidden = swapped(hidden, "face")
    pieces = partner(face_id, jnp.arange(n_face, dtype=jnp.int32), n_face)
    first_cycle = tile_id * cycle_dev + (face_id // n_sub) * cyc_own
    parity = (first_cycle + jnp.arange(cyc_own, dtype=jnp.int32)) % 2
    coeffs = cycle_spectrum(hidden, pieces, parity, pixels, degrees)
    tall = pixels // LANES
    coeffs = coeffs.reshape(cyc_own * 2, degrees, samples * sub)
    coeffs = jnp.concatenate(list(coeffs), axis=1)
    order_map = jnp.roll(order_map, -chan_id * owners * slot_dev)
    place = (order_map % tall) * (degrees // tall) + order_map // tall
    picking = (place[:, None] == jnp.arange(degrees, dtype=jnp.int32)[None, :]).astype(jnp.bfloat16)
    coeffs = jnp.dot(picking, coeffs, preferred_element_type=jnp.float32).astype(jnp.bfloat16)
    width = 2 * samples * sub
    coeffs = coeffs.reshape(n_chan, owners, chunks, per, ROWS, cyc_own, width)
    coeffs = coeffs.transpose(0, 2, 1, 3, 5, 4, 6)
    coeffs = coeffs.reshape(n_chan, chunks, owners, per, cyc_own * ROWS, width)
    turns = [coeffs[0]]
    for k in range(1, n_chan):
        pairs = [((i + k) % n_chan, i) for i in range(n_chan)]
        turns.append(lax.ppermute(coeffs[n_chan - k], "chan", pairs))
    coeffs = jnp.stack(turns)

    if late < chunks:
        across = lax.all_gather(coeffs[:, late], "face", axis=0, tiled=False)
    lines = [along_tiles(coeffs[:, :1])]
    if chunks > 1:
        lines.append(along_tiles(coeffs[:, 1:late]))
    out = None
    for chunk in range(chunks):
        if chunk == late:
            got = along_tiles(across)
        else:
            line = lines[0][:, :, 0] if chunk == 0 else lines[1][:, :, chunk - 1]
            got = lax.all_gather(line, "face", axis=0, tiled=False)
        if n_sub > 1:
            got = got.reshape(n_cyc, n_sub, n_tile, n_chan, owners, per, cyc_own * ROWS, width)
            got = got.transpose(0, 2, 3, 4, 5, 6, 1, 7)
        got = got.reshape(n_cyc * n_tile, n_chan, owners, per, cyc_own * ROWS, n_sub * width)
        out = mix(got, fetched[chunk], weights, out, chunk, chunks, sub)
    return out.reshape(owners * slot_dev, 2, samples, degree_dev, chan_dev * n_chan)


def solution(mesh):
    in_specs = (
        P(None, "chan", "tile", "face"),
        P(),
        P(),
        P(("chan", "face", "tile"), None, None),
        P(("face", "tile"), None, None),
    )
    out_specs = P("chan", None, None, ("face", "tile"), None)
    return jax.shard_map(body, mesh=mesh, in_specs=in_specs, out_specs=out_specs, check_vma=False)
```

time: 578 us -> 527 us (0.912)
  waiting for transfers between devices: 307 us -> 180 us
  starting transfers between devices: 27.6 us -> 106 us
  local copies, waits for them, and re-layouts: 63.2 us -> 14.9 us
  blocking collectives: 4.58 us -> 51.9 us
  Pallas kernels: 121 us -> 104 us
  other arithmetic: 12 us -> 22 us
    all_to_all x5 -> x4, waiting for transfers between devices: 199 us -> 21.3 us  [body(): lax.all_to_all(tables.pop(0), ('face', 'tile'), split_axis=0, concat_axis...]
    ppermute x4 -> x26, waiting for transfers between devices: 22.7 us -> 149 us  [the longest x9 90.4 us: along_tiles(): falling.append(lax.ppermute(falling[-1], 'tile', down))]
    ppermute x4 -> x26, starting transfers between devices: 6.8 us -> 81.3 us  [the longest x9 57.3 us: along_tiles(): rising.append(lax.ppermute(rising[-1], 'tile', up))]
    all_gather x5, waiting for transfers between devices: 83 us -> 9.6 us  [the longest x1 9.58 us: body(): padded = lax.all_gather(padded, 'chan', axis=1, tiled=True)]
    all_to_all x1, blocking collectives: 4.58 us -> 51.9 us  [body(): lax.all_to_all(tables.pop(0), ('face', 'tile'), split_axis=0, concat_axis...]
    pallas_call x4, Pallas kernels: 121 us -> 93.7 us  [mix(): pl.pallas_call(run, grid=(src // srcs,), in_specs=in_specs, out_specs=pl....]
    slice x8 -> x7, local copies, waits for them, and re-layouts: 22.1 us -> 3.33 us  [the longest x1 1.69 us: body(): line = lines[0][:, :, 0] if chunk == 0 else lines[1][:, :, chunk - 1]]
    another operation x0 -> x15, other arithmetic: none -> 14.3 us  [the longest x13 12.7 us: along_tiles(): return jnp.stack(parts)]
  transfers between devices with their start and end apart: 14 -> 35, of which waited for: 11 -> 18; matrix products, arithmetic and copies ran while one was open for 9% -> 5% of each run, Pallas kernels for 16% -> 16%
where the time goes in v2:
time: 527 us; the launch traced here: 516 us
  waiting for transfers between devices  180 us (34%)
  starting transfers between devices  106 us (20%)
  Pallas kernels  104 us (20%)
  blocking collectives  51.9 us (10%)
  matrix products  23.1 us (4%)
  other arithmetic  22 us (4%)
  local copies, waits for them, and re-layouts  14.9 us (3%)
  between operations  13.8 us (3%)
    pallas_call x4, Pallas kernels, mix(): pl.pallas_call(run, grid=(src // srcs,), in_specs=in_specs, out_specs=pl....  93.7 us
    ppermute x9, waiting for transfers between devices, along_tiles(): falling.append(lax.ppermute(falling[-1], 'tile', down))  90.4 us
    ppermute x9, starting transfers between devices, along_tiles(): rising.append(lax.ppermute(rising[-1], 'tile', up))  57.3 us
    all_to_all x1, blocking collectives, body(): lax.all_to_all(tables.pop(0), ('face', 'tile'), split_axis=0, concat_axis...  51.9 us
    ppermute x9, waiting for transfers between devices, along_tiles(): rising.append(lax.ppermute(rising[-1], 'tile', up))  36.4 us
    all_to_all x4, starting transfers between devices, body(): lax.all_to_all(tables.pop(0), ('face', 'tile'), split_axis=0, concat_axis...  24.8 us
    all_to_all x4, waiting for transfers between devices, body(): lax.all_to_all(tables.pop(0), ('face', 'tile'), split_axis=0, concat_axis...  21.3 us
    another operation x13, other arithmetic, along_tiles(): return jnp.stack(parts)  12.7 us
  transfers between devices with their start and end apart: 35, of which 18 were waited for; matrix products, arithmetic and copies ran while one was open for 5% of the time, Pallas kernels for 16%

profile of v2, /device:TPU:0, one launch (start us, length us, event | category | flops | bytes accessed | tf_op | source)
XLA Modules:
  0.0 516.1 jit_solution(4515561552509091809)
XLA Ops:
  6.5 1.8 copy.40
  8.4 5.0 collective-permute-start
  16.3 4.0 collective-permute-done.1
  20.4 2.5 collective-permute-start.3
  24.4 3.1 collective-permute-done.2
  27.7 2.5 concatenate.29
  31.0 9.6 %all-gather.10.cloned.1.call-done = bf16[1,128,10,1026]{3,1,2,0:T(8,128)(2,1)} async-done(((bf16[1,64,10,1026]{3,1,2,0:T(8,128)(2,1)}), bf16[1,128,10,1026]{3,1,2,0:T(8,128)(2,1)}) %all-gather.10.cloned.1.call-update) | async-done | bytes 2626576 | tf_op jit(solution)/shard_map/all_gather | solution.py:314
  40.6 2.7 fusion.9
  50.2 1.8 collective-permute-start.4
  54.0 5.5 %collective-permute-done.4 = bf16[2,64,1024]{2,1,0:T(8,128)(2,1)S(1)} collective-permute-done((bf16[2,64,1024]{2,1,0:T(8,128)(2,1)S(1)}, bf16[2,64,1024]{2,1,0:T(8,128)(2,1)S(1)}, u32[]{:S(2)}, u32[]{:S(2)}) %collective-permute-start.4) | collective-permute-done | bytes 262176 | tf_op jit(solution)/shard_map/ppermute | solution.py:164
  59.5 6.4 %collective-permute-done.5 = bf16[2,64,1024]{2,1,0:T(8,128)(2,1)S(1)} collective-permute-done((bf16[2,64,1024]{2,1,0:T(8,128)(2,1)S(1)}, bf16[2,64,1024]{2,1,0:T(8,128)(2,1)S(1)}, u32[]{:S(2)}, u32[]{:S(2)}) %collective-permute-start.5) | collective-permute-done | bytes 262176 | tf_op jit(solution)/shard_map/ppermute | solution.py:164
  65.9 1.8 convolution_bitcast_fusion
  69.1 8.1 %bitcast_convert_fusion = bf16[2,2,64,32,64]{4,2,3,1,0:T(8,128)(2,1)S(1)} fusion(f32[2,32,2,64,128,1]{4,1,3,2,0,5:T(8,128)S(1)} %maximum_bitcast_fusion, f32[1,2,2,128,64]{3,4,0,1,2:T(8,128)S(1)} %get-tuple-element.40, f32[1,2,2,128,64]{3,4,0,1,2:T(8,128)S(1)} %get-tuple-element.39), kind=kOutput, calls=%fused_computation.8 | convolution fusion | flops 1611202560 | bytes 5505024 | tf_op jit(solution)/shard_map/imrxb,izrbk->rzmkx/dot_general | solution.py:73
  77.3 3.8 fusion.5
  81.4 1.8 collective-permute-done.7
  85.4 4.6 collective-permute-start.20
  90.0 4.4 collective-permute-done.21
  95.7 4.6 collective-permute-start.24
  100.2 3.5 collective-permute-done.22
  105.0 4.6 collective-permute-start.25
  109.7 2.6 collective-permute-done.23
  117.1 3.4 copy-done.2
  120.5 10.1 %tables.1 = (bf16[16,2,128,256]{3,2,1,0:T(8,128)(2,1)S(1)}, bf16[16,1,128,256]{3,2,1,0:T(8,128)(2,1)}, bf16[16,1,128,256]{3,2,1,0:T(8,128)(2,1)}, bf16[16,2,128,...) custom-call(bf16[64,32,2048]{2,1,0:T(8,128)(2,1)S(1)} %copy-done.2, s32[8,1,256]{2,1,0:T(1,128)S(1)} %tile.13.order_ref), custom_call_target="tpu_custom_call" | custom-call | flops 2147483648 | bytes 16777216 | tf_op jit(solution)/shard_map/tables/pallas_call | solution.py:113
  130.6 9.0 %all-to-all-start.2 = ((bf16[16,1,128,256]{3,2,1,0:T(8,128)(2,1)}), bf16[16,1,128,256]{3,2,1,0:T(8,128)(2,1)}, u32[]{:S(2)}, u32[]{:S(2)}) async-start(bf16[16,1,128,256]{3,2,1,0:T(8,128)(2,1)} %get-tuple-element.12), calls=%async_computation.2 | async-start | bytes 2097152 | tf_op jit(solution)/shard_map/all_to_all | solution.py:322
  139.6 3.8 collective-permute-start.14
  144.7 20.1 %collective-permute-done.14 = bf16[2,2,16,2,16,128]{5,4,3,2,1,0:T(8,128)(2,1)S(1)} collective-permute-done((bf16[2,2,16,2,16,128]{5,4,3,2,1,0:T(8,128)(2,1)}, bf16[2,2,16,2,16,128]{5,4,3,2,1,0:T(8,128)(2,1)S(1)}, u32[]{:S(2)}, u32[]{:S(2)}) %collective-permute-start.14) | collective-permute-done | bytes 524320 | tf_op jit(solution)/shard_map/ppermute | solution.py:175
  164.8 9.1 %collective-permute-start.18 = (bf16[2,2,16,2,16,128]{5,4,3,2,1,0:T(8,128)(2,1)S(1)}, bf16[2,2,16,2,16,128]{5,4,3,2,1,0:T(8,128)(2,1)S(1)}, u32[]{:S(2)}, u32[]{:S(2)}) collective-permute-start(bf16[2,2,16,2,16,128]{5,4,3,2,1,0:T(8,128)(2,1)S(1)} %collective-permute-done.14), channel_id=1, source_target_pairs={{0,1},{1,2},{2,3},{4,5},{5,6},{6,7},{8,9},{9,10},{10,11},{12,13},{... | collective-permute-start | bytes 1572872 | tf_op jit(solution)/shard_map/ppermute | solution.py:175
  176.1 7.7 %collective-permute-done.18 = bf16[2,2,16,2,16,128]{5,4,3,2,1,0:T(8,128)(2,1)S(1)} collective-permute-done((bf16[2,2,16,2,16,128]{5,4,3,2,1,0:T(8,128)(2,1)S(1)}, bf16[2,2,16,2,16,128]{5,4,3,2,1,0:T(8,128)(2,1)S(1)}, u32[]{:S(2)}, u32[]{:S(2)}) %collective-permute-start.18) | collective-permute-done | bytes 524320 | tf_op jit(solution)/shard_map/ppermute | solution.py:175
  183.8 4.4 collective-permute-start.19
  189.9 7.4 %collective-permute-done.19 = bf16[2,2,16,2,16,128]{5,4,3,2,1,0:T(8,128)(2,1)S(1)} collective-permute-done((bf16[2,2,16,2,16,128]{5,4,3,2,1,0:T(8,128)(2,1)S(1)}, bf16[2,2,16,2,16,128]{5,4,3,2,1,0:T(8,128)(2,1)S(1)}, u32[]{:S(2)}, u32[]{:S(2)}) %collective-permute-start.19) | collective-permute-done | bytes 524320 | tf_op jit(solution)/shard_map/ppermute | solution.py:175
  197.4 1.9 select_bitcast_fusion.3
  199.3 7.7 %all-to-all-start.3 = ((bf16[16,1,128,256]{3,2,1,0:T(8,128)(2,1)}), bf16[16,1,128,256]{3,2,1,0:T(8,128)(2,1)S(1)}, u32[]{:S(2)}, u32[]{:S(2)}) async-start(bf16[16,1,128,256]{3,2,1,0:T(8,128)(2,1)} %get-tuple-element.13), calls=%async_computation.3 | async-start | bytes 2097152 | tf_op jit(solution)/shard_map/all_to_all | solution.py:322
  210.5 21.3 %all-to-all-done.3.refs_3_ = bf16[16,1,128,256]{3,2,1,0:T(8,128)(2,1)S(1)} async-done(((bf16[16,1,128,256]{3,2,1,0:T(8,128)(2,1)}), bf16[16,1,128,256]{3,2,1,0:T(8,128)(2,1)S(1)}, u32[]{:S(2)}, u32[]{:S(2)}) %all-to-all-start.3) | async-done | bytes 1048608 | tf_op jit(solution)/shard_map/all_to_all | solution.py:322
  231.8 51.9 %all_to_all.25.refs_0_ = bf16[16,2,128,256]{3,2,1,0:T(8,128)(2,1)} all-to-all(bf16[16,2,128,256]{3,2,1,0:T(8,128)(2,1)S(1)} %get-tuple-element.14), channel_id=1, replica_groups=mesh['chan'=2,'face'=4,'tile'=4] {'face','tile'}, dimensions={0} | all-to-all | bytes 4194304 | tf_op jit(solution)/shard_map/all_to_all | solution.py:322
  283.8 3.7 all-to-all-start.1
  289.4 4.8 collective-permute-start.8
  294.2 50.8 %collective-permute-done.9 = bf16[4,2,16,2,16,128]{5,4,3,2,1,0:T(8,128)(2,1)S(1)} collective-permute-done((bf16[4,2,16,2,16,128]{5,4,3,2,1,0:T(8,128)(2,1)}, bf16[4,2,16,2,16,128]{5,4,3,2,1,0:T(8,128)(2,1)S(1)}, u32[]{:S(2)}, u32[]{:S(2)}) %collective-permute-start.9) | collective-permute-done | bytes 1048608 | tf_op jit(solution)/shard_map/ppermute | solution.py:176
  346.4 16.0 %collective-permute-start.12 = (bf16[4,2,16,2,16,128]{5,4,3,2,1,0:T(8,128)(2,1)S(1)}, bf16[4,2,16,2,16,128]{5,4,3,2,1,0:T(8,128)(2,1)}, u32[]{:S(2)}, u32[]{:S(2)}) collective-permute-start(bf16[4,2,16,2,16,128]{5,4,3,2,1,0:T(8,128)(2,1)S(1)} %collective-permute-done.8), channel_id=1, source_target_pairs={{0,1},{1,2},{2,3},{4,5},{5,6},{6,7},{8,9},{9,10},{10,11},{12,13},{... | collective-permute-start | bytes 3145736 | tf_op jit(solution)/shard_map/ppermute | solution.py:175
  362.4 19.5 %collective-permute-done.10 = bf16[4,2,16,2,16,128]{5,4,3,2,1,0:T(8,128)(2,1)} collective-permute-done((bf16[4,2,16,2,16,128]{5,4,3,2,1,0:T(8,128)(2,1)S(1)}, bf16[4,2,16,2,16,128]{5,4,3,2,1,0:T(8,128)(2,1)}, u32[]{:S(2)}, u32[]{:S(2)}) %collective-permute-start.10) | collective-permute-done | bytes 1048608 | tf_op jit(solution)/shard_map/ppermute | solution.py:176
  383.2 5.5 %collective-permute-start.13 = (bf16[4,2,16,2,16,128]{5,4,3,2,1,0:T(8,128)(2,1)}, bf16[4,2,16,2,16,128]{5,4,3,2,1,0:T(8,128)(2,1)}, u32[]{:S(2)}, u32[]{:S(2)}) collective-permute-start(bf16[4,2,16,2,16,128]{5,4,3,2,1,0:T(8,128)(2,1)} %collective-permute-done.12), channel_id=1, source_target_pairs={{0,1},{1,2},{2,3},{4,5},{5,6},{6,7},{8,9},{9,10},{10,11},{12,13},{... | collective-permute-start | bytes 3145736 | tf_op jit(solution)/shard_map/ppermute | solution.py:175
  390.1 4.4 all-to-all-start
  394.6 5.4 %fusion.2.w_ref.refs_1_ = bf16[128,128,128]{2,1,0:T(8,128)(2,1)} fusion(s32[]{:T(128)S(6)} %select_n.198, bf16[128,128,128]{2,1,0:T(8,128)(2,1)} %param.9), kind=kLoop, calls=%fused_computation.5 | loop fusion | flops 8388608 | bytes 8388612 | tf_op jit(solution)/shard_map/jit(_roll_dynamic)/concatenate | solution.py:311
  401.4 9.6 %collective-permute-done.11 = bf16[4,2,16,2,16,128]{5,4,3,2,1,0:T(8,128)(2,1)} collective-permute-done((bf16[4,2,16,2,16,128]{5,4,3,2,1,0:T(8,128)(2,1)}, bf16[4,2,16,2,16,128]{5,4,3,2,1,0:T(8,128)(2,1)}, u32[]{:S(2)}, u32[]{:S(2)}) %collective-permute-start.11) | collective-permute-done | bytes 1048608 | tf_op jit(solution)/shard_map/ppermute | solution.py:176
  413.6 2.3 pad_maximum_fusion
  415.8 23.4 %mix.4.refs_4_ = bf16[16,4,16,2,128,128]{5,4,3,2,1,0:T(8,128)(2,1)} custom-call(bf16[16,2,16,2,16,128]{5,4,3,2,1,0:T(8,128)(2,1)} %bitcast.235, bf16[128,128,128]{2,1,0:T(8,128)(2,1)} %fusion.2.w_ref.refs_1_, bf16[16,2,128,256]{3,2,1,0:T(8,128)(2,1)} %all_to_all.25.refs_0_), custom_call_target="tpu_custom_call" | custom-call | flops 8589934592 | bytes 27262976 | tf_op jit(solution)/shard_map/mix/pallas_call | solution.py:259
  439.3 23.4 %mix.5.refs_3_ = bf16[16,4,16,2,128,128]{5,4,3,2,1,0:T(8,128)(2,1)} custom-call(bf16[16,2,16,2,16,128]{5,4,3,2,1,0:T(8,128)(2,1)} %bitcast.236, bf16[128,128,128]{2,1,0:T(8,128)(2,1)} %fusion.2.w_ref.refs_1_, bf16[16,1,128,256]{3,2,1,0:T(8,128)(2,1)} %all-to-all-done.2.refs_2_, bf16[16,1,128,256]{3,2,1,0:T(8,128)(2,1)} %copy-done.5, ...), custom_call_target="tpu_custom_call", output_to_operand_aliasing={{}: (4, {})} | custom-call | flops 8589934592 | bytes 27262976 | tf_op jit(solution)/shard_map/mix/pallas_call | solution.py:259
  462.7 23.4 %mix.6.refs_3_ = bf16[16,4,16,2,128,128]{5,4,3,2,1,0:T(8,128)(2,1)} custom-call(bf16[16,2,16,2,16,128]{5,4,3,2,1,0:T(8,128)(2,1)} %bitcast.237, bf16[128,128,128]{2,1,0:T(8,128)(2,1)} %fusion.2.w_ref.refs_1_, bf16[16,2,128,256]{3,2,1,0:T(8,128)(2,1)} %copy-done.4, bf16[16,4,16,2,128,128]{5,4,3,2,1,0:T(8,128)(2,1)} %mix.5.refs_3_), custom_call_target="tpu_custom_call", output_to_operand_aliasing={{}: (3, {})} | custom-call | flops 8589934592 | bytes 27262976 | tf_op jit(solution)/shard_map/mix/pallas_call | solution.py:259
  486.1 23.5 %mix.7 = bf16[16,4,16,2,128,128]{5,4,3,2,1,0:T(8,128)(2,1)} custom-call(bf16[16,2,16,2,16,128]{5,4,3,2,1,0:T(8,128)(2,1)} %bitcast.227, bf16[128,128,128]{2,1,0:T(8,128)(2,1)} %fusion.2.w_ref.refs_1_, bf16[16,2,128,256]{3,2,1,0:T(8,128)(2,1)} %all-to-all-done.refs_2_, bf16[16,4,16,2,128,128]{5,4,3,2,1,0:T(8,128)(2,1)} %mix.6.refs_3_), custom_call_target="tpu_custom_call", output_to_operand_aliasing={{}: (3, {})} | custom-call | flops 8589934592 | bytes 27262976 | tf_op jit(solution)/shard_map/mix/pallas_call | solution.py:259
  (121 shorter events, 44.3 us)
Async XLA Ops:
  6.5 34.0 %copy-start = (bf16[3,3,128,128]{3,2,1,0:T(8,128)(2,1)S(1)}, bf16[3,3,128,128]{3,2,1,0:T(8,128)(2,1)}, u32[]{:S(2)}) copy-start(bf16[3,3,128,128]{3,2,1,0:T(8,128)(2,1)} %param.6) | copy-start | bytes 884740
  6.5 34.0 %all-gather.10.cloned.1.call-start = ((), (), s32[]{:S(2)}) async-start(), calls=%async_computation.5 | async-start | bytes 4423680 | tf_op jit(solution)/shard_map/all_gather | solution.py:314
  8.4 7.7 %collective-permute-start = (bf16[1,64,1024]{2,1,0:T(8,128)(2,1)S(1)}, bf16[1,64,1024]{2,1,0:T(8,128)(2,1)S(1)}, u32[]{:S(2)}, u32[]{:S(2)}) collective-permute-start(bf16[1,64,1024]{2,1,0:T(8,128)(2,1)S(1)} %get-tuple-element.37), channel_id=1, source_target_pairs={{0,1},{1,2},{2,3},{4,5},{5,6},{6,7},{8,9},{9,10},{10,11},{12,13},{... | collective-permute-start | bytes 393224 | tf_op jit(solution)/shard_map/ppermute | solution.py:20
  13.4 6.9 %collective-permute-start.1 = (bf16[1,64,1024]{2,1,0:T(8,128)(2,1)S(1)}, bf16[1,64,1024]{2,1,0:T(8,128)(2,1)S(1)}, u32[]{:S(2)}, u32[]{:S(2)}) collective-permute-start(bf16[1,64,1024]{2,1,0:T(8,128)(2,1)S(1)} %get-tuple-element.38), channel_id=1, source_target_pairs={{1,0},{2,1},{3,2},{5,4},{6,5},{7,6},{9,8},{10,9},{11,10},{13,12},{... | collective-permute-start | bytes 393224 | tf_op jit(solution)/shard_map/ppermute | solution.py:21
  20.4 3.8 collective-permute-start.3
  23.0 4.6 collective-permute-start.2
  30.2 257.9 %all-gather.12.cloned.1.call-start = ((), (), s32[]{:S(2)}) async-start(), calls=%async_computation.6 | async-start | bytes 1310720 | tf_op jit(solution)/shard_map/all_gather | solution.py:354
  40.6 2.7 copy-start.3
  50.1 3.7 copy-start.9
  50.2 9.2 %collective-permute-start.4 = (bf16[2,64,1024]{2,1,0:T(8,128)(2,1)S(1)}, bf16[2,64,1024]{2,1,0:T(8,128)(2,1)S(1)}, u32[]{:S(2)}, u32[]{:S(2)}) collective-permute-start(bf16[2,64,1024]{2,1,0:T(8,128)(2,1)S(1)} %get-tuple-element.34), channel_id=1, source_target_pairs={{0,4},{4,0},{8,12},{12,8},{1,5},{5,1},{9,13},{13,9},{2,6},{6,2},{1... | collective-permute-start | bytes 786440 | tf_op jit(solution)/shard_map/ppermute | solution.py:164
  52.0 13.8 %collective-permute-start.5 = (bf16[2,64,1024]{2,1,0:T(8,128)(2,1)S(1)}, bf16[2,64,1024]{2,1,0:T(8,128)(2,1)S(1)}, u32[]{:S(2)}, u32[]{:S(2)}) collective-permute-start(bf16[2,64,1024]{2,1,0:T(8,128)(2,1)S(1)} %get-tuple-element.33), channel_id=1, source_target_pairs={{0,8},{4,12},{8,0},{12,4},{1,9},{5,13},{9,1},{13,5},{2,10},{6,14},... | collective-permute-start | bytes 786440 | tf_op jit(solution)/shard_map/ppermute | solution.py:164
  53.5 12.4 %collective-permute-start.6 = (bf16[2,64,1024]{2,1,0:T(8,128)(2,1)S(1)}, bf16[2,64,1024]{2,1,0:T(8,128)(2,1)S(1)}, u32[]{:S(2)}, u32[]{:S(2)}) collective-permute-start(bf16[2,64,1024]{2,1,0:T(8,128)(2,1)S(1)} %get-tuple-element.32), channel_id=1, source_target_pairs={{0,12},{4,8},{8,4},{12,0},{1,13},{5,9},{9,5},{13,1},{2,14},{6,10},... | collective-permute-start | bytes 786440 | tf_op jit(solution)/shard_map/ppermute | solution.py:164
  81.3 2.0 collective-permute-start.7
  84.1 331.8 %all-gather.18.cloned.1.call-start = ((), (), s32[]{:S(2)}) async-start(), calls=%async_computation.9 | async-start | bytes 5242880 | tf_op jit(solution)/shard_map/all_gather | solution.py:364
  84.1 10.2 %collective-permute-start.21 = (bf16[2,1,16,2,16,128]{5,4,3,2,1,0:T(8,128)(2,1)S(1)}, bf16[2,1,16,2,16,128]{5,4,3,2,1,0:T(8,128)(2,1)S(1)}, u32[]{:S(2)}, u32[]{:S(2)}) collective-permute-start(bf16[2,1,16,2,16,128]{5,4,3,2,1,0:T(8,128)(2,1)S(1)} %get-tuple-element.27), channel_id=1, source_target_pairs={{1,0},{2,1},{3,2},{5,4},{6,5},{7,6},{9,8},{10,9},{11,10},{13,12},{... | collective-permute-start | bytes 786440 | tf_op jit(solution)/shard_map/ppermute | solution.py:176
  85.4 10.2 %collective-permute-start.20 = (bf16[2,1,16,2,16,128]{5,4,3,2,0,1:T(8,128)(2,1)S(1)}, bf16[2,1,16,2,16,128]{5,4,3,2,0,1:T(8,128)(2,1)S(1)}, u32[]{:S(2)}, u32[]{:S(2)}) collective-permute-start(bf16[2,1,16,2,16,128]{5,4,3,2,0,1:T(8,128)(2,1)S(1)} %bitcast.245), channel_id=1, source_target_pairs={{0,1},{1,2},{2,3},{4,5},{5,6},{6,7},{8,9},{9,10},{10,11},{12,13},{... | collective-permute-start | bytes 786440 | tf_op jit(solution)/shard_map/ppermute | solution.py:175
  94.4 9.4 %collective-permute-start.22 = (bf16[2,1,16,2,16,128]{5,4,3,2,0,1:T(8,128)(2,1)S(1)}, bf16[2,1,16,2,16,128]{5,4,3,2,0,1:T(8,128)(2,1)S(1)}, u32[]{:S(2)}, u32[]{:S(2)}) collective-permute-start(bf16[2,1,16,2,16,128]{5,4,3,2,0,1:T(8,128)(2,1)S(1)} %bitcast.254), channel_id=1, source_target_pairs={{1,0},{2,1},{3,2},{5,4},{6,5},{7,6},{9,8},{10,9},{11,10},{13,12},{... | collective-permute-start | bytes 786440 | tf_op jit(solution)/shard_map/ppermute | solution.py:176
  95.7 9.4 %collective-permute-start.24 = (bf16[2,1,16,2,16,128]{5,4,3,2,0,1:T(8,128)(2,1)S(1)}, bf16[2,1,16,2,16,128]{5,4,3,2,0,1:T(8,128)(2,1)S(1)}, u32[]{:S(2)}, u32[]{:S(2)}) collective-permute-start(bf16[2,1,16,2,16,128]{5,4,3,2,0,1:T(8,128)(2,1)S(1)} %collective-permute-done.20), channel_id=1, source_target_pairs={{0,1},{1,2},{2,3},{4,5},{5,6},{6,7},{8,9},{9,10},{10,11},{12,13},{... | collective-permute-start | bytes 786440 | tf_op jit(solution)/shard_map/ppermute | solution.py:175
  103.7 8.5 %collective-permute-start.23 = (bf16[2,1,16,2,16,128]{5,4,3,2,0,1:T(8,128)(2,1)S(1)}, bf16[2,1,16,2,16,128]{5,4,3,2,0,1:T(8,128)(2,1)S(1)}, u32[]{:S(2)}, u32[]{:S(2)}) collective-permute-start(bf16[2,1,16,2,16,128]{5,4,3,2,0,1:T(8,128)(2,1)S(1)} %collective-permute-done.22), channel_id=1, source_target_pairs={{1,0},{2,1},{3,2},{5,4},{6,5},{7,6},{9,8},{10,9},{11,10},{13,12},{... | collective-permute-start | bytes 786440 | tf_op jit(solution)/shard_map/ppermute | solution.py:176
  105.0 8.4 %collective-permute-start.25 = (bf16[2,1,16,2,16,128]{5,4,3,2,0,1:T(8,128)(2,1)S(1)}, bf16[2,1,16,2,16,128]{5,4,3,2,0,1:T(8,128)(2,1)S(1)}, u32[]{:S(2)}, u32[]{:S(2)}) collective-permute-start(bf16[2,1,16,2,16,128]{5,4,3,2,0,1:T(8,128)(2,1)S(1)} %collective-permute-done.24), channel_id=1, source_target_pairs={{0,1},{1,2},{2,3},{4,5},{5,6},{6,7},{8,9},{9,10},{10,11},{12,13},{... | collective-permute-start | bytes 786440 | tf_op jit(solution)/shard_map/ppermute | solution.py:175
  115.8 27.6 %collective-permute-start.15 = (bf16[2,2,16,2,16,128]{5,4,3,2,1,0:T(8,128)(2,1)}, bf16[2,2,16,2,16,128]{5,4,3,2,1,0:T(8,128)(2,1)}, u32[]{:S(2)}, u32[]{:S(2)}) collective-permute-start(bf16[2,2,16,2,16,128]{5,4,3,2,1,0:T(8,128)(2,1)} %fusion.30), channel_id=1, source_target_pairs={{1,0},{2,1},{3,2},{5,4},{6,5},{7,6},{9,8},{10,9},{11,10},{13,12},{... | collective-permute-start | bytes 1572872 | tf_op jit(solution)/shard_map/ppermute | solution.py:176
  117.1 3.4 copy-start.2
  130.6 68.7 %all-to-all-start.2 = ((bf16[16,1,128,256]{3,2,1,0:T(8,128)(2,1)}), bf16[16,1,128,256]{3,2,1,0:T(8,128)(2,1)}, u32[]{:S(2)}, u32[]{:S(2)}) async-start(bf16[16,1,128,256]{3,2,1,0:T(8,128)(2,1)} %get-tuple-element.12), calls=%async_computation.2 | async-start | bytes 2097152 | tf_op jit(solution)/shard_map/all_to_all | solution.py:322
  139.6 25.2 %collective-permute-start.14 = (bf16[2,2,16,2,16,128]{5,4,3,2,1,0:T(8,128)(2,1)}, bf16[2,2,16,2,16,128]{5,4,3,2,1,0:T(8,128)(2,1)S(1)}, u32[]{:S(2)}, u32[]{:S(2)}) collective-permute-start(bf16[2,2,16,2,16,128]{5,4,3,2,1,0:T(8,128)(2,1)} %fusion.30), channel_id=1, source_target_pairs={{0,1},{1,2},{2,3},{4,5},{5,6},{6,7},{8,9},{9,10},{10,11},{12,13},{... | collective-permute-start | bytes 1572872 | tf_op jit(solution)/shard_map/ppermute | solution.py:175
  143.4 30.5 %collective-permute-start.16 = (bf16[2,2,16,2,16,128]{5,4,3,2,1,0:T(8,128)(2,1)}, bf16[2,2,16,2,16,128]{5,4,3,2,1,0:T(8,128)(2,1)S(1)}, u32[]{:S(2)}, u32[]{:S(2)}) collective-permute-start(bf16[2,2,16,2,16,128]{5,4,3,2,1,0:T(8,128)(2,1)} %collective-permute-done.15), channel_id=1, source_target_pairs={{1,0},{2,1},{3,2},{5,4},{6,5},{7,6},{9,8},{10,9},{11,10},{13,12},{... | collective-permute-start | bytes 1572872 | tf_op jit(solution)/shard_map/ppermute | solution.py:176
  164.8 19.0 %collective-permute-start.18 = (bf16[2,2,16,2,16,128]{5,4,3,2,1,0:T(8,128)(2,1)S(1)}, bf16[2,2,16,2,16,128]{5,4,3,2,1,0:T(8,128)(2,1)S(1)}, u32[]{:S(2)}, u32[]{:S(2)}) collective-permute-start(bf16[2,2,16,2,16,128]{5,4,3,2,1,0:T(8,128)(2,1)S(1)} %collective-permute-done.14), channel_id=1, source_target_pairs={{0,1},{1,2},{2,3},{4,5},{5,6},{6,7},{8,9},{9,10},{10,11},{12,13},{... | collective-permute-start | bytes 1572872 | tf_op jit(solution)/shard_map/ppermute | solution.py:175
  173.9 15.2 %collective-permute-start.17 = (bf16[2,2,16,2,16,128]{5,4,3,2,1,0:T(8,128)(2,1)S(1)}, bf16[2,2,16,2,16,128]{5,4,3,2,1,0:T(8,128)(2,1)S(1)}, u32[]{:S(2)}, u32[]{:S(2)}) collective-permute-start(bf16[2,2,16,2,16,128]{5,4,3,2,1,0:T(8,128)(2,1)S(1)} %collective-permute-done.16), channel_id=1, source_target_pairs={{1,0},{2,1},{3,2},{5,4},{6,5},{7,6},{9,8},{10,9},{11,10},{13,12},{... | collective-permute-start | bytes 1572872 | tf_op jit(solution)/shard_map/ppermute | solution.py:176
  183.8 13.6 %collective-permute-start.19 = (bf16[2,2,16,2,16,128]{5,4,3,2,1,0:T(8,128)(2,1)S(1)}, bf16[2,2,16,2,16,128]{5,4,3,2,1,0:T(8,128)(2,1)S(1)}, u32[]{:S(2)}, u32[]{:S(2)}) collective-permute-start(bf16[2,2,16,2,16,128]{5,4,3,2,1,0:T(8,128)(2,1)S(1)} %collective-permute-done.18), channel_id=1, source_target_pairs={{0,1},{1,2},{2,3},{4,5},{5,6},{6,7},{8,9},{9,10},{10,11},{12,13},{... | collective-permute-start | bytes 1572872 | tf_op jit(solution)/shard_map/ppermute | solution.py:175
  199.3 32.5 %all-to-all-start.3 = ((bf16[16,1,128,256]{3,2,1,0:T(8,128)(2,1)}), bf16[16,1,128,256]{3,2,1,0:T(8,128)(2,1)S(1)}, u32[]{:S(2)}, u32[]{:S(2)}) async-start(bf16[16,1,128,256]{3,2,1,0:T(8,128)(2,1)} %get-tuple-element.13), calls=%async_computation.3 | async-start | bytes 2097152 | tf_op jit(solution)/shard_map/all_to_all | solution.py:322
  207.0 232.3 %all-gather.16.cloned.1.call-start = ((), (), s32[]{:S(2)}) async-start(), calls=%async_computation.8 | async-start | bytes 5242880 | tf_op jit(solution)/shard_map/all_gather | solution.py:364
  231.8 51.9 %copy-start.5 = (bf16[16,1,128,256]{3,2,1,0:T(8,128)(2,1)}, bf16[16,1,128,256]{3,2,1,0:T(8,128)(2,1)S(1)}, u32[]{:S(2)}) copy-start(bf16[16,1,128,256]{3,2,1,0:T(8,128)(2,1)S(1)} %all-to-all-done.3.refs_3_) | copy-start | bytes 3145732
  283.8 104.9 %all-to-all-start.1 = ((bf16[16,2,128,256]{3,2,1,0:T(8,128)(2,1)}), bf16[16,2,128,256]{3,2,1,0:T(8,128)(2,1)S(1)}, u32[]{:S(2)}, u32[]{:S(2)}) async-start(bf16[16,2,128,256]{3,2,1,0:T(8,128)(2,1)} %get-tuple-element.11), calls=%async_computation.1 | async-start | bytes 4194304 | tf_op jit(solution)/shard_map/all_to_all | solution.py:322
  287.5 175.2 %all-gather.14.cloned.1.call-start = ((), (), s32[]{:S(2)}) async-start(), calls=%async_computation.7 | async-start | bytes 5242880 | tf_op jit(solution)/shard_map/all_gather | solution.py:364
  288.1 57.0 %collective-permute-start.9 = (bf16[4,2,16,2,16,128]{5,4,3,2,1,0:T(8,128)(2,1)}, bf16[4,2,16,2,16,128]{5,4,3,2,1,0:T(8,128)(2,1)S(1)}, u32[]{:S(2)}, u32[]{:S(2)}) collective-permute-start(bf16[4,2,16,2,16,128]{5,4,3,2,1,0:T(8,128)(2,1)} %bitcast.247), channel_id=1, source_target_pairs={{1,0},{2,1},{3,2},{5,4},{6,5},{7,6},{9,8},{10,9},{11,10},{13,12},{... | collective-permute-start | bytes 3145736 | tf_op jit(solution)/shard_map/ppermute | solution.py:176
  289.4 57.0 %collective-permute-start.8 = (bf16[4,2,16,2,16,128]{5,4,3,2,1,0:T(8,128)(2,1)}, bf16[4,2,16,2,16,128]{5,4,3,2,1,0:T(8,128)(2,1)S(1)}, u32[]{:S(2)}, u32[]{:S(2)}) collective-permute-start(bf16[4,2,16,2,16,128]{5,4,3,2,1,0:T(8,128)(2,1)} %bitcast.248), channel_id=1, source_target_pairs={{0,1},{1,2},{2,3},{4,5},{5,6},{6,7},{8,9},{9,10},{10,11},{12,13},{... | collective-permute-start | bytes 3145736 | tf_op jit(solution)/shard_map/ppermute | solution.py:175
  345.1 36.8 %collective-permute-start.10 = (bf16[4,2,16,2,16,128]{5,4,3,2,1,0:T(8,128)(2,1)S(1)}, bf16[4,2,16,2,16,128]{5,4,3,2,1,0:T(8,128)(2,1)}, u32[]{:S(2)}, u32[]{:S(2)}) collective-permute-start(bf16[4,2,16,2,16,128]{5,4,3,2,1,0:T(8,128)(2,1)S(1)} %collective-permute-done.9), channel_id=1, source_target_pairs={{1,0},{2,1},{3,2},{5,4},{6,5},{7,6},{9,8},{10,9},{11,10},{13,12},{... | collective-permute-start | bytes 3145736 | tf_op jit(solution)/shard_map/ppermute | solution.py:176
  346.4 35.5 %copy-start.6 = (bf16[4,2,16,2,16,128]{5,4,3,2,1,0:T(8,128)(2,1)}, bf16[4,2,16,2,16,128]{5,4,3,2,1,0:T(8,128)(2,1)S(1)}, u32[]{:S(2)}) copy-start(bf16[4,2,16,2,16,128]{5,4,3,2,1,0:T(8,128)(2,1)S(1)} %collective-permute-done.8) | copy-start | bytes 3145732
  346.4 36.8 %collective-permute-start.12 = (bf16[4,2,16,2,16,128]{5,4,3,2,1,0:T(8,128)(2,1)S(1)}, bf16[4,2,16,2,16,128]{5,4,3,2,1,0:T(8,128)(2,1)}, u32[]{:S(2)}, u32[]{:S(2)}) collective-permute-start(bf16[4,2,16,2,16,128]{5,4,3,2,1,0:T(8,128)(2,1)S(1)} %collective-permute-done.8), channel_id=1, source_target_pairs={{0,1},{1,2},{2,3},{4,5},{5,6},{6,7},{8,9},{9,10},{10,11},{12,13},{... | collective-permute-start | bytes 3145736 | tf_op jit(solution)/shard_map/ppermute | solution.py:175
  381.9 29.1 %collective-permute-start.11 = (bf16[4,2,16,2,16,128]{5,4,3,2,1,0:T(8,128)(2,1)}, bf16[4,2,16,2,16,128]{5,4,3,2,1,0:T(8,128)(2,1)}, u32[]{:S(2)}, u32[]{:S(2)}) collective-permute-start(bf16[4,2,16,2,16,128]{5,4,3,2,1,0:T(8,128)(2,1)} %collective-permute-done.10), channel_id=1, source_target_pairs={{1,0},{2,1},{3,2},{5,4},{6,5},{7,6},{9,8},{10,9},{11,10},{13,12},{... | collective-permute-start | bytes 3145736 | tf_op jit(solution)/shard_map/ppermute | solution.py:176
  383.2 29.2 %collective-permute-start.13 = (bf16[4,2,16,2,16,128]{5,4,3,2,1,0:T(8,128)(2,1)}, bf16[4,2,16,2,16,128]{5,4,3,2,1,0:T(8,128)(2,1)}, u32[]{:S(2)}, u32[]{:S(2)}) collective-permute-start(bf16[4,2,16,2,16,128]{5,4,3,2,1,0:T(8,128)(2,1)} %collective-permute-done.12), channel_id=1, source_target_pairs={{0,1},{1,2},{2,3},{4,5},{5,6},{6,7},{8,9},{9,10},{10,11},{12,13},{... | collective-permute-start | bytes 3145736 | tf_op jit(solution)/shard_map/ppermute | solution.py:175
  388.7 1.4 copy-start.4
  390.1 96.0 %all-to-all-start = ((bf16[16,2,128,256]{3,2,1,0:T(8,128)(2,1)}), bf16[16,2,128,256]{3,2,1,0:T(8,128)(2,1)}, u32[]{:S(2)}, u32[]{:S(2)}) async-start(bf16[16,2,128,256]{3,2,1,0:T(8,128)(2,1)} %get-tuple-element.10), calls=%async_computation | async-start | bytes 4194304 | tf_op jit(solution)/shard_map/all_to_all | solution.py:322
  399.9 11.1 %copy-start.7 = (bf16[4,2,16,2,16,128]{5,4,3,2,1,0:T(8,128)(2,1)S(1)}, bf16[4,2,16,2,16,128]{5,4,3,2,1,0:T(8,128)(2,1)}, u32[]{:S(2)}) copy-start(bf16[4,2,16,2,16,128]{5,4,3,2,1,0:T(8,128)(2,1)} %copy-done.6) | copy-start | bytes 3145732
  412.4 1.2 copy-start.8
  486.1 23.5 %copy-start.1 = (bf16[3,3,128,128]{3,2,1,0:T(8,128)(2,1)S(1)}, bf16[3,3,128,128]{3,2,1,0:T(8,128)(2,1)}, u32[]{:S(2)}) copy-start(bf16[3,3,128,128]{3,2,1,0:T(8,128)(2,1)} %param.6) | copy-start | bytes 884740
Sparse Core Ops, SparseCore 0:
  30.4 10.1 all-gather.9
  84.2 26.4 all-gather.11
  114.8 59.2 all-gather.17
  210.7 71.0 all-gather.15
  289.8 68.9 all-gather.13

commit v3 on v2

--- a/solution.py
+++ b/solution.py
@@ -171,12 +171,23 @@
     up = [(i, i + 1) for i in range(n_tile - 1)]
     down = [(i + 1, i) for i in range(n_tile - 1)]
     rising, falling = [piece], [piece]
-    for _ in range(n_tile - 1):
+    for _ in range(n_tile - 2):
         rising.append(lax.ppermute(rising[-1], "tile", up))
         falling.append(lax.ppermute(falling[-1], "tile", down))
+    ends = lax.ppermute(piece, "tile", [(0, n_tile - 1), (n_tile - 1, 0)])
+    rising.append(ends)
+    falling.append(ends)
     parts = [piece]
     for k in range(1, n_tile):
         parts.append(jnp.where(tile_id >= k, rising[k], falling[n_tile - k]))
+    return jnp.stack(parts)
+
+
+def around_tiles(piece):
+    n_tile = lax.axis_size("tile")
+    parts = [piece]
+    for k in range(1, n_tile):
+        parts.append(lax.ppermute(piece, "tile", [(i, (i + k) % n_tile) for i in range(n_tile)]))
     return jnp.stack(parts)
 
 
@@ -308,10 +319,10 @@
     else:
         tables = plain_tables(legendre, own_orders, n_face, n_tile, n_cyc, cyc_own)
         tables = jnp.split(tables, list(np.cumsum(sum(sizes, []))[:-1]), axis=1)
-    weights = jnp.roll(spectral_weight, -chan_id * chan_dev, axis=1)
 
     padded = extended(field)
     padded = lax.all_gather(padded, "chan", axis=1, tiled=True)
+    weights = jnp.roll(spectral_weight, -chan_id * chan_dev, axis=1)
 
     fetched = []
     tables = list(tables)
@@ -352,7 +363,7 @@
 
     if late < chunks:
         across = lax.all_gather(coeffs[:, late], "face", axis=0, tiled=False)
-    lines = [along_tiles(coeffs[:, :1])]
+    lines = [around_tiles(coeffs[:, :1])]
     if chunks > 1:
         lines.append(along_tiles(coeffs[:, 1:late]))
     out = None

time: 527 us -> 522 us (level)
  the two profiles are of different devices: /device:TPU:0 before, /device:TPU:12 now
where the time goes in v3:
time: 522 us; the launch traced here: 521 us
  waiting for transfers between devices  221 us (42%)
  Pallas kernels  104 us (20%)
  starting transfers between devices  68.9 us (13%)
  blocking collectives  53.5 us (10%)
  matrix products  23.1 us (4%)
  other arithmetic  23 us (4%)
  local copies, waits for them, and re-layouts  13.8 us (3%)
  between operations  13.7 us (3%)
    ppermute x4, waiting for transfers between devices, along_tiles(): rising.append(lax.ppermute(rising[-1], 'tile', up))  138 us
    pallas_call x4, Pallas kernels, mix(): pl.pallas_call(run, grid=(src // srcs,), in_specs=in_specs, out_specs=pl....  93.7 us
    all_to_all x1, blocking collectives, body(): lax.all_to_all(tables.pop(0), ('face', 'tile'), split_axis=0, concat_axis...  53.5 us
    all_to_all x4, starting transfers between devices, body(): lax.all_to_all(tables.pop(0), ('face', 'tile'), split_axis=0, concat_axis...  23.2 us
    ppermute x3, waiting for transfers between devices, around_tiles(): lax.ppermute(piece, 'tile', [(i, (i + k) % n_tile) for i in range(n_tile)])  21.7 us
    all_to_all x4, waiting for transfers between devices, body(): lax.all_to_all(tables.pop(0), ('face', 'tile'), split_axis=0, concat_axis...  19.1 us
    ppermute x4, starting transfers between devices, along_tiles(): rising.append(lax.ppermute(rising[-1], 'tile', up))  15.5 us
    another operation x7, other arithmetic, along_tiles(): return jnp.stack(parts)  12.7 us
  transfers between devices with their start and end apart: 30, of which 17 were waited for; matrix products, arithmetic and copies ran while one was open for 5% of the time, Pallas kernels for 15%

profile of v3, /device:TPU:12, one launch (start us, length us, event | category | flops | bytes accessed | tf_op | source)
XLA Modules:
  0.0 520.9 jit_solution(2423331664223659871)
XLA Ops:
  6.5 1.8 copy.40
  8.4 3.5 collective-permute-start
  11.9 2.4 collective-permute-start.1
  15.9 2.9 collective-permute-done.1
  22.8 2.2 collective-permute-done.2
  25.2 2.5 concatenate.29
  28.5 10.7 %all-gather.10.cloned.1.call-done = bf16[1,128,10,1026]{3,1,2,0:T(8,128)(2,1)} async-done(((bf16[1,64,10,1026]{3,1,2,0:T(8,128)(2,1)}), bf16[1,128,10,1026]{3,1,2,0:T(8,128)(2,1)}) %all-gather.10.cloned.1.call-update) | async-done | bytes 2626576 | tf_op jit(solution)/shard_map/all_gather | solution.py:324
  39.2 2.7 fusion.9
  52.6 5.5 %collective-permute-done.4 = bf16[2,64,1024]{2,1,0:T(8,128)(2,1)S(1)} collective-permute-done((bf16[2,64,1024]{2,1,0:T(8,128)(2,1)S(1)}, bf16[2,64,1024]{2,1,0:T(8,128)(2,1)S(1)}, u32[]{:S(2)}, u32[]{:S(2)}) %collective-permute-start.4) | collective-permute-done | bytes 262176 | tf_op jit(solution)/shard_map/ppermute | solution.py:164
  58.1 6.1 %collective-permute-done.5 = bf16[2,64,1024]{2,1,0:T(8,128)(2,1)S(1)} collective-permute-done((bf16[2,64,1024]{2,1,0:T(8,128)(2,1)S(1)}, bf16[2,64,1024]{2,1,0:T(8,128)(2,1)S(1)}, u32[]{:S(2)}, u32[]{:S(2)}) %collective-permute-start.5) | collective-permute-done | bytes 262176 | tf_op jit(solution)/shard_map/ppermute | solution.py:164
  64.3 1.8 convolution_bitcast_fusion
  67.5 8.1 %bitcast_convert_fusion = bf16[2,2,64,32,64]{4,2,3,1,0:T(8,128)(2,1)S(1)} fusion(f32[2,32,2,64,128,1]{4,1,3,2,0,5:T(8,128)S(1)} %maximum_bitcast_fusion, f32[1,2,2,128,64]{3,4,0,1,2:T(8,128)S(1)} %get-tuple-element.44, f32[1,2,2,128,64]{3,4,0,1,2:T(8,128)S(1)} %get-tuple-element.43), kind=kOutput, calls=%fused_computation.8 | convolution fusion | flops 1611202560 | bytes 5505024 | tf_op jit(solution)/shard_map/imrxb,izrbk->rzmkx/dot_general | solution.py:73
  75.7 3.8 fusion.5
  79.8 1.8 collective-permute-done.7
  87.0 14.8 %collective-permute-done.18 = bf16[2,1,16,2,16,128]{5,4,3,2,0,1:T(8,128)(2,1)S(1)} collective-permute-done((bf16[2,1,16,2,16,128]{5,4,3,2,0,1:T(8,128)(2,1)S(1)}, bf16[2,1,16,2,16,128]{5,4,3,2,0,1:T(8,128)(2,1)S(1)}, u32[]{:S(2)}, u32[]{:S(2)}) %collective-permute-start.18) | collective-permute-done | bytes 262176 | tf_op jit(solution)/shard_map/ppermute | solution.py:190
  101.8 4.9 collective-permute-done.19
  106.8 1.9 collective-permute-done.20
  110.1 3.4 copy-done.2
  113.5 10.1 %tables.1 = (bf16[16,2,128,256]{3,2,1,0:T(8,128)(2,1)S(1)}, bf16[16,1,128,256]{3,2,1,0:T(8,128)(2,1)}, bf16[16,1,128,256]{3,2,1,0:T(8,128)(2,1)}, bf16[16,2,128,...) custom-call(bf16[64,32,2048]{2,1,0:T(8,128)(2,1)S(1)} %copy-done.2, s32[8,1,256]{2,1,0:T(1,128)S(1)} %tile.13.order_ref), custom_call_target="tpu_custom_call" | custom-call | flops 2147483648 | bytes 16777216 | tf_op jit(solution)/shard_map/tables/pallas_call | solution.py:113
  123.6 5.1 all-to-all-start.2
  129.5 3.4 collective-permute-start.13
  132.9 3.3 collective-permute-start.16
  137.6 35.5 %collective-permute-done.13 = bf16[2,2,16,2,16,128]{5,4,3,2,1,0:T(8,128)(2,1)} collective-permute-done((bf16[2,2,16,2,16,128]{5,4,3,2,1,0:T(8,128)(2,1)}, bf16[2,2,16,2,16,128]{5,4,3,2,1,0:T(8,128)(2,1)}, u32[]{:S(2)}, u32[]{:S(2)}) %collective-permute-start.13) | collective-permute-done | bytes 524320 | tf_op jit(solution)/shard_map/ppermute | solution.py:175
  173.2 4.4 collective-permute-start.15
  177.6 2.3 collective-permute-start.17
  180.7 2.5 select_bitcast_fusion.5
  183.2 6.0 %collective-permute-done.15 = bf16[2,2,16,2,16,128]{5,4,3,2,1,0:T(8,128)(2,1)} collective-permute-done((bf16[2,2,16,2,16,128]{5,4,3,2,1,0:T(8,128)(2,1)}, bf16[2,2,16,2,16,128]{5,4,3,2,1,0:T(8,128)(2,1)}, u32[]{:S(2)}, u32[]{:S(2)}) %collective-permute-start.15) | collective-permute-done | bytes 524320 | tf_op jit(solution)/shard_map/ppermute | solution.py:175
  189.2 4.1 collective-permute-done.17
  193.3 1.9 select_bitcast_fusion.4
  195.2 5.1 all-to-all-start.3
  203.8 19.1 %all-to-all-done.3.refs_3_ = bf16[16,1,128,256]{3,2,1,0:T(8,128)(2,1)S(1)} async-done(((bf16[16,1,128,256]{3,2,1,0:T(8,128)(2,1)}), bf16[16,1,128,256]{3,2,1,0:T(8,128)(2,1)S(1)}, u32[]{:S(2)}, u32[]{:S(2)}) %all-to-all-start.3) | async-done | bytes 1048608 | tf_op jit(solution)/shard_map/all_to_all | solution.py:333
  222.9 53.5 %all_to_all.25.refs_0_ = bf16[16,2,128,256]{3,2,1,0:T(8,128)(2,1)} all-to-all(bf16[16,2,128,256]{3,2,1,0:T(8,128)(2,1)S(1)} %get-tuple-element.14), channel_id=1, replica_groups=mesh['chan'=2,'face'=4,'tile'=4] {'face','tile'}, dimensions={0} | all-to-all | bytes 4194304 | tf_op jit(solution)/shard_map/all_to_all | solution.py:333
  276.5 6.6 %all-to-all-start.1 = ((bf16[16,2,128,256]{3,2,1,0:T(8,128)(2,1)}), bf16[16,2,128,256]{3,2,1,0:T(8,128)(2,1)S(1)}, u32[]{:S(2)}, u32[]{:S(2)}) async-start(bf16[16,2,128,256]{3,2,1,0:T(8,128)(2,1)} %get-tuple-element.11), calls=%async_computation.1 | async-start | bytes 4194304 | tf_op jit(solution)/shard_map/all_to_all | solution.py:333
  283.7 3.4 collective-permute-start.8
  287.1 3.4 collective-permute-start.11
  292.2 80.8 %collective-permute-done.8 = bf16[4,2,16,2,16,128]{5,4,3,2,1,0:T(8,128)(2,1)} collective-permute-done((bf16[4,2,16,2,16,128]{5,4,3,2,1,0:T(8,128)(2,1)}, bf16[4,2,16,2,16,128]{5,4,3,2,1,0:T(8,128)(2,1)}, u32[]{:S(2)}, u32[]{:S(2)}) %collective-permute-start.8) | collective-permute-done | bytes 1048608 | tf_op jit(solution)/shard_map/ppermute | solution.py:175
  373.0 4.4 collective-permute-start.10
  377.4 1.9 collective-permute-start.12
  380.7 6.3 %all-to-all-start = ((bf16[16,2,128,256]{3,2,1,0:T(8,128)(2,1)}), bf16[16,2,128,256]{3,2,1,0:T(8,128)(2,1)}, u32[]{:S(2)}, u32[]{:S(2)}) async-start(bf16[16,2,128,256]{3,2,1,0:T(8,128)(2,1)} %get-tuple-element.10), calls=%async_computation | async-start | bytes 4194304 | tf_op jit(solution)/shard_map/all_to_all | solution.py:333
  387.0 5.3 %fusion.2.w_ref.refs_1_ = bf16[128,128,128]{2,1,0:T(8,128)(2,1)} fusion(s32[]{:T(128)S(6)} %select_n.178, bf16[128,128,128]{2,1,0:T(8,128)(2,1)} %param.9), kind=kLoop, calls=%fused_computation.5 | loop fusion | flops 8388608 | bytes 8388612 | tf_op jit(solution)/shard_map/jit(_roll_dynamic)/concatenate | solution.py:325
  392.4 2.0 select_bitcast_fusion.2
  394.4 15.4 %collective-permute-done.10 = bf16[4,2,16,2,16,128]{5,4,3,2,1,0:T(8,128)(2,1)S(1)} collective-permute-done((bf16[4,2,16,2,16,128]{5,4,3,2,1,0:T(8,128)(2,1)}, bf16[4,2,16,2,16,128]{5,4,3,2,1,0:T(8,128)(2,1)S(1)}, u32[]{:S(2)}, u32[]{:S(2)}) %collective-permute-start.10) | collective-permute-done | bytes 1048608 | tf_op jit(solution)/shard_map/ppermute | solution.py:175
  409.9 7.1 %collective-permute-done.12 = bf16[4,2,16,2,16,128]{5,4,3,2,1,0:T(8,128)(2,1)} collective-permute-done((bf16[4,2,16,2,16,128]{5,4,3,2,1,0:T(8,128)(2,1)}, bf16[4,2,16,2,16,128]{5,4,3,2,1,0:T(8,128)(2,1)}, u32[]{:S(2)}, u32[]{:S(2)}) %collective-permute-start.12) | collective-permute-done | bytes 1048608 | tf_op jit(solution)/shard_map/ppermute | solution.py:176
  418.3 2.3 pad_maximum_fusion
  420.6 23.4 %mix.4.refs_4_ = bf16[16,4,16,2,128,128]{5,4,3,2,1,0:T(8,128)(2,1)} custom-call(bf16[16,2,16,2,16,128]{5,4,3,2,1,0:T(8,128)(2,1)} %bitcast.228, bf16[128,128,128]{2,1,0:T(8,128)(2,1)} %fusion.2.w_ref.refs_1_, bf16[16,2,128,256]{3,2,1,0:T(8,128)(2,1)} %all_to_all.25.refs_0_), custom_call_target="tpu_custom_call" | custom-call | flops 8589934592 | bytes 27262976 | tf_op jit(solution)/shard_map/mix/pallas_call | solution.py:270
  444.0 23.4 %mix.5.refs_3_ = bf16[16,4,16,2,128,128]{5,4,3,2,1,0:T(8,128)(2,1)} custom-call(bf16[16,2,16,2,16,128]{5,4,3,2,1,0:T(8,128)(2,1)} %bitcast.229, bf16[128,128,128]{2,1,0:T(8,128)(2,1)} %fusion.2.w_ref.refs_1_, bf16[16,1,128,256]{3,2,1,0:T(8,128)(2,1)} %all-to-all-done.2.refs_2_, bf16[16,1,128,256]{3,2,1,0:T(8,128)(2,1)} %copy-done.5, ...), custom_call_target="tpu_custom_call", output_to_operand_aliasing={{}: (4, {})} | custom-call | flops 8589934592 | bytes 27262976 | tf_op jit(solution)/shard_map/mix/pallas_call | solution.py:270
  467.4 23.4 %mix.6.refs_3_ = bf16[16,4,16,2,128,128]{5,4,3,2,1,0:T(8,128)(2,1)} custom-call(bf16[16,2,16,2,16,128]{5,4,3,2,1,0:T(8,128)(2,1)} %bitcast.230, bf16[128,128,128]{2,1,0:T(8,128)(2,1)} %fusion.2.w_ref.refs_1_, bf16[16,2,128,256]{3,2,1,0:T(8,128)(2,1)} %copy-done.4, bf16[16,4,16,2,128,128]{5,4,3,2,1,0:T(8,128)(2,1)} %mix.5.refs_3_), custom_call_target="tpu_custom_call", output_to_operand_aliasing={{}: (3, {})} | custom-call | flops 8589934592 | bytes 27262976 | tf_op jit(solution)/shard_map/mix/pallas_call | solution.py:270
  490.9 23.5 %mix.7 = bf16[16,4,16,2,128,128]{5,4,3,2,1,0:T(8,128)(2,1)} custom-call(bf16[16,2,16,2,16,128]{5,4,3,2,1,0:T(8,128)(2,1)} %bitcast.220, bf16[128,128,128]{2,1,0:T(8,128)(2,1)} %fusion.2.w_ref.refs_1_, bf16[16,2,128,256]{3,2,1,0:T(8,128)(2,1)} %all-to-all-done.refs_2_, bf16[16,4,16,2,128,128]{5,4,3,2,1,0:T(8,128)(2,1)} %mix.6.refs_3_), custom_call_target="tpu_custom_call", output_to_operand_aliasing={{}: (3, {})} | custom-call | flops 8589934592 | bytes 27262976 | tf_op jit(solution)/shard_map/mix/pallas_call | solution.py:270
  (102 shorter events, 37.2 us)
Async XLA Ops:
  6.5 32.7 %copy-start = (bf16[3,3,128,128]{3,2,1,0:T(8,128)(2,1)S(1)}, bf16[3,3,128,128]{3,2,1,0:T(8,128)(2,1)}, u32[]{:S(2)}) copy-start(bf16[3,3,128,128]{3,2,1,0:T(8,128)(2,1)} %param.6) | copy-start | bytes 884740
  6.5 32.7 %all-gather.10.cloned.1.call-start = ((), (), s32[]{:S(2)}) async-start(), calls=%async_computation.5 | async-start | bytes 4423680 | tf_op jit(solution)/shard_map/all_gather | solution.py:324
  8.4 7.3 %collective-permute-start = (bf16[1,64,1024]{2,1,0:T(8,128)(2,1)S(1)}, bf16[1,64,1024]{2,1,0:T(8,128)(2,1)S(1)}, u32[]{:S(2)}, u32[]{:S(2)}) collective-permute-start(bf16[1,64,1024]{2,1,0:T(8,128)(2,1)S(1)} %get-tuple-element.39), channel_id=1, source_target_pairs={{0,1},{1,2},{2,3},{4,5},{5,6},{6,7},{8,9},{9,10},{10,11},{12,13},{... | collective-permute-start | bytes 393224 | tf_op jit(solution)/shard_map/ppermute | solution.py:20
  11.9 6.9 %collective-permute-start.1 = (bf16[1,64,1024]{2,1,0:T(8,128)(2,1)S(1)}, bf16[1,64,1024]{2,1,0:T(8,128)(2,1)S(1)}, u32[]{:S(2)}, u32[]{:S(2)}) collective-permute-start(bf16[1,64,1024]{2,1,0:T(8,128)(2,1)S(1)} %get-tuple-element.40), channel_id=1, source_target_pairs={{1,0},{2,1},{3,2},{5,4},{6,5},{7,6},{9,8},{10,9},{11,10},{13,12},{... | collective-permute-start | bytes 393224 | tf_op jit(solution)/shard_map/ppermute | solution.py:21
  19.0 3.7 collective-permute-start.3
  20.5 4.6 collective-permute-start.2
  27.7 256.0 %all-gather.12.cloned.1.call-start = ((), (), s32[]{:S(2)}) async-start(), calls=%async_computation.6 | async-start | bytes 1310720 | tf_op jit(solution)/shard_map/all_gather | solution.py:365
  39.2 2.7 copy-start.3
  48.7 3.7 copy-start.7
  48.8 9.2 %collective-permute-start.4 = (bf16[2,64,1024]{2,1,0:T(8,128)(2,1)S(1)}, bf16[2,64,1024]{2,1,0:T(8,128)(2,1)S(1)}, u32[]{:S(2)}, u32[]{:S(2)}) collective-permute-start(bf16[2,64,1024]{2,1,0:T(8,128)(2,1)S(1)} %get-tuple-element.36), channel_id=1, source_target_pairs={{0,4},{4,0},{8,12},{12,8},{1,5},{5,1},{9,13},{13,9},{2,6},{6,2},{1... | collective-permute-start | bytes 786440 | tf_op jit(solution)/shard_map/ppermute | solution.py:164
  50.4 13.8 %collective-permute-start.5 = (bf16[2,64,1024]{2,1,0:T(8,128)(2,1)S(1)}, bf16[2,64,1024]{2,1,0:T(8,128)(2,1)S(1)}, u32[]{:S(2)}, u32[]{:S(2)}) collective-permute-start(bf16[2,64,1024]{2,1,0:T(8,128)(2,1)S(1)} %get-tuple-element.35), channel_id=1, source_target_pairs={{0,8},{4,12},{8,0},{12,4},{1,9},{5,13},{9,1},{13,5},{2,10},{6,14},... | collective-permute-start | bytes 786440 | tf_op jit(solution)/shard_map/ppermute | solution.py:164
  50.9 13.3 %collective-permute-start.6 = (bf16[2,64,1024]{2,1,0:T(8,128)(2,1)S(1)}, bf16[2,64,1024]{2,1,0:T(8,128)(2,1)S(1)}, u32[]{:S(2)}, u32[]{:S(2)}) collective-permute-start(bf16[2,64,1024]{2,1,0:T(8,128)(2,1)S(1)} %get-tuple-element.34), channel_id=1, source_target_pairs={{0,12},{4,8},{8,4},{12,0},{1,13},{5,9},{9,5},{13,1},{2,14},{6,10},... | collective-permute-start | bytes 786440 | tf_op jit(solution)/shard_map/ppermute | solution.py:164
  79.7 2.0 collective-permute-start.7
  82.5 338.1 %all-gather.18.cloned.1.call-start = ((), (), s32[]{:S(2)}) async-start(), calls=%async_computation.9 | async-start | bytes 5242880 | tf_op jit(solution)/shard_map/all_gather | solution.py:375
  82.5 19.3 %collective-permute-start.18 = (bf16[2,1,16,2,16,128]{5,4,3,2,0,1:T(8,128)(2,1)S(1)}, bf16[2,1,16,2,16,128]{5,4,3,2,0,1:T(8,128)(2,1)S(1)}, u32[]{:S(2)}, u32[]{:S(2)}) collective-permute-start(bf16[2,1,16,2,16,128]{5,4,3,2,0,1:T(8,128)(2,1)S(1)} %bitcast.238), channel_id=1, source_target_pairs={{0,1},{1,2},{2,3},{3,0},{4,5},{5,6},{6,7},{7,4},{8,9},{9,10},{10,1... | collective-permute-start | bytes 786440 | tf_op jit(solution)/shard_map/ppermute | solution.py:190
  84.0 22.7 %collective-permute-start.19 = (bf16[2,1,16,2,16,128]{5,4,3,2,0,1:T(8,128)(2,1)S(1)}, bf16[2,1,16,2,16,128]{5,4,3,2,0,1:T(8,128)(2,1)S(1)}, u32[]{:S(2)}, u32[]{:S(2)}) collective-permute-start(bf16[2,1,16,2,16,128]{5,4,3,2,0,1:T(8,128)(2,1)S(1)} %bitcast.239), channel_id=1, source_target_pairs={{0,2},{1,3},{2,0},{3,1},{4,6},{5,7},{6,4},{7,5},{8,10},{9,11},{10,... | collective-permute-start | bytes 786440 | tf_op jit(solution)/shard_map/ppermute | solution.py:190
  85.5 23.2 %collective-permute-start.20 = (bf16[2,1,16,2,16,128]{5,4,3,2,1,0:T(8,128)(2,1)S(1)}, bf16[2,1,16,2,16,128]{5,4,3,2,1,0:T(8,128)(2,1)S(1)}, u32[]{:S(2)}, u32[]{:S(2)}) collective-permute-start(bf16[2,1,16,2,16,128]{5,4,3,2,1,0:T(8,128)(2,1)S(1)} %get-tuple-element.27), channel_id=1, source_target_pairs={{0,3},{1,0},{2,1},{3,2},{4,7},{5,4},{6,5},{7,6},{8,11},{9,8},{10,9... | collective-permute-start | bytes 786440 | tf_op jit(solution)/shard_map/ppermute | solution.py:190
  110.1 3.4 copy-start.2
  123.6 71.7 %all-to-all-start.2 = ((bf16[16,1,128,256]{3,2,1,0:T(8,128)(2,1)}), bf16[16,1,128,256]{3,2,1,0:T(8,128)(2,1)}, u32[]{:S(2)}, u32[]{:S(2)}) async-start(bf16[16,1,128,256]{3,2,1,0:T(8,128)(2,1)} %get-tuple-element.12), calls=%async_computation.2 | async-start | bytes 2097152 | tf_op jit(solution)/shard_map/all_to_all | solution.py:333
  129.5 43.6 %collective-permute-start.13 = (bf16[2,2,16,2,16,128]{5,4,3,2,1,0:T(8,128)(2,1)}, bf16[2,2,16,2,16,128]{5,4,3,2,1,0:T(8,128)(2,1)}, u32[]{:S(2)}, u32[]{:S(2)}) collective-permute-start(bf16[2,2,16,2,16,128]{5,4,3,2,1,0:T(8,128)(2,1)} %fusion.30), channel_id=1, source_target_pairs={{0,1},{1,2},{2,3},{4,5},{5,6},{6,7},{8,9},{9,10},{10,11},{12,13},{... | collective-permute-start | bytes 1572872 | tf_op jit(solution)/shard_map/ppermute | solution.py:175
  132.9 44.6 %collective-permute-start.16 = (bf16[2,2,16,2,16,128]{5,4,3,2,1,0:T(8,128)(2,1)}, bf16[2,2,16,2,16,128]{5,4,3,2,1,0:T(8,128)(2,1)}, u32[]{:S(2)}, u32[]{:S(2)}) collective-permute-start(bf16[2,2,16,2,16,128]{5,4,3,2,1,0:T(8,128)(2,1)} %fusion.30), channel_id=1, source_target_pairs={{1,0},{2,1},{3,2},{5,4},{6,5},{7,6},{9,8},{10,9},{11,10},{13,12},{... | collective-permute-start | bytes 1572872 | tf_op jit(solution)/shard_map/ppermute | solution.py:176
  136.2 44.5 %collective-permute-start.14 = (bf16[2,2,16,2,16,128]{5,4,3,2,1,0:T(8,128)(2,1)}, bf16[2,2,16,2,16,128]{5,4,3,2,1,0:T(8,128)(2,1)}, u32[]{:S(2)}, u32[]{:S(2)}) collective-permute-start(bf16[2,2,16,2,16,128]{5,4,3,2,1,0:T(8,128)(2,1)} %fusion.30), channel_id=1, source_target_pairs={{0,3},{3,0},{4,7},{7,4},{8,11},{11,8},{12,15},{15,12},{16,19},{19,... | collective-permute-start | bytes 1572872 | tf_op jit(solution)/shard_map/ppermute | solution.py:177
  173.2 16.0 %collective-permute-start.15 = (bf16[2,2,16,2,16,128]{5,4,3,2,1,0:T(8,128)(2,1)}, bf16[2,2,16,2,16,128]{5,4,3,2,1,0:T(8,128)(2,1)}, u32[]{:S(2)}, u32[]{:S(2)}) collective-permute-start(bf16[2,2,16,2,16,128]{5,4,3,2,1,0:T(8,128)(2,1)} %collective-permute-done.13), channel_id=1, source_target_pairs={{0,1},{1,2},{2,3},{4,5},{5,6},{6,7},{8,9},{9,10},{10,11},{12,13},{... | collective-permute-start | bytes 1572872 | tf_op jit(solution)/shard_map/ppermute | solution.py:175
  177.6 15.8 %collective-permute-start.17 = (bf16[2,2,16,2,16,128]{5,4,3,2,1,0:T(8,128)(2,1)}, bf16[2,2,16,2,16,128]{5,4,3,2,1,0:T(8,128)(2,1)}, u32[]{:S(2)}, u32[]{:S(2)}) collective-permute-start(bf16[2,2,16,2,16,128]{5,4,3,2,1,0:T(8,128)(2,1)} %collective-permute-done.16), channel_id=1, source_target_pairs={{1,0},{2,1},{3,2},{5,4},{6,5},{7,6},{9,8},{10,9},{11,10},{13,12},{... | collective-permute-start | bytes 1572872 | tf_op jit(solution)/shard_map/ppermute | solution.py:176
  195.2 27.7 %all-to-all-start.3 = ((bf16[16,1,128,256]{3,2,1,0:T(8,128)(2,1)}), bf16[16,1,128,256]{3,2,1,0:T(8,128)(2,1)S(1)}, u32[]{:S(2)}, u32[]{:S(2)}) async-start(bf16[16,1,128,256]{3,2,1,0:T(8,128)(2,1)} %get-tuple-element.13), calls=%async_computation.3 | async-start | bytes 2097152 | tf_op jit(solution)/shard_map/all_to_all | solution.py:333
  200.3 243.7 %all-gather.16.cloned.1.call-start = ((), (), s32[]{:S(2)}) async-start(), calls=%async_computation.8 | async-start | bytes 5242880 | tf_op jit(solution)/shard_map/all_gather | solution.py:375
  222.9 53.5 %copy-start.5 = (bf16[16,1,128,256]{3,2,1,0:T(8,128)(2,1)}, bf16[16,1,128,256]{3,2,1,0:T(8,128)(2,1)S(1)}, u32[]{:S(2)}) copy-start(bf16[16,1,128,256]{3,2,1,0:T(8,128)(2,1)S(1)} %all-to-all-done.3.refs_3_) | copy-start | bytes 3145732
  276.5 102.9 %all-to-all-start.1 = ((bf16[16,2,128,256]{3,2,1,0:T(8,128)(2,1)}), bf16[16,2,128,256]{3,2,1,0:T(8,128)(2,1)S(1)}, u32[]{:S(2)}, u32[]{:S(2)}) async-start(bf16[16,2,128,256]{3,2,1,0:T(8,128)(2,1)} %get-tuple-element.11), calls=%async_computation.1 | async-start | bytes 4194304 | tf_op jit(solution)/shard_map/all_to_all | solution.py:333
  283.1 184.3 %all-gather.14.cloned.1.call-start = ((), (), s32[]{:S(2)}) async-start(), calls=%async_computation.7 | async-start | bytes 5242880 | tf_op jit(solution)/shard_map/all_gather | solution.py:375
  283.7 89.3 %collective-permute-start.8 = (bf16[4,2,16,2,16,128]{5,4,3,2,1,0:T(8,128)(2,1)}, bf16[4,2,16,2,16,128]{5,4,3,2,1,0:T(8,128)(2,1)}, u32[]{:S(2)}, u32[]{:S(2)}) collective-permute-start(bf16[4,2,16,2,16,128]{5,4,3,2,1,0:T(8,128)(2,1)} %bitcast.241), channel_id=1, source_target_pairs={{0,1},{1,2},{2,3},{4,5},{5,6},{6,7},{8,9},{9,10},{10,11},{12,13},{... | collective-permute-start | bytes 3145736 | tf_op jit(solution)/shard_map/ppermute | solution.py:175
  287.1 90.3 %collective-permute-start.11 = (bf16[4,2,16,2,16,128]{5,4,3,2,1,0:T(8,128)(2,1)}, bf16[4,2,16,2,16,128]{5,4,3,2,1,0:T(8,128)(2,1)}, u32[]{:S(2)}, u32[]{:S(2)}) collective-permute-start(bf16[4,2,16,2,16,128]{5,4,3,2,1,0:T(8,128)(2,1)} %bitcast.242), channel_id=1, source_target_pairs={{1,0},{2,1},{3,2},{5,4},{6,5},{7,6},{9,8},{10,9},{11,10},{13,12},{... | collective-permute-start | bytes 3145736 | tf_op jit(solution)/shard_map/ppermute | solution.py:176
  290.6 101.8 %collective-permute-start.9 = (bf16[4,2,16,2,16,128]{5,4,3,2,1,0:T(8,128)(2,1)}, bf16[4,2,16,2,16,128]{5,4,3,2,1,0:T(8,128)(2,1)}, u32[]{:S(2)}, u32[]{:S(2)}) collective-permute-start(bf16[4,2,16,2,16,128]{5,4,3,2,1,0:T(8,128)(2,1)} %bitcast.243), channel_id=1, source_target_pairs={{0,3},{3,0},{4,7},{7,4},{8,11},{11,8},{12,15},{15,12},{16,19},{19,... | collective-permute-start | bytes 3145736 | tf_op jit(solution)/shard_map/ppermute | solution.py:177
  373.0 36.8 %collective-permute-start.10 = (bf16[4,2,16,2,16,128]{5,4,3,2,1,0:T(8,128)(2,1)}, bf16[4,2,16,2,16,128]{5,4,3,2,1,0:T(8,128)(2,1)S(1)}, u32[]{:S(2)}, u32[]{:S(2)}) collective-permute-start(bf16[4,2,16,2,16,128]{5,4,3,2,1,0:T(8,128)(2,1)} %collective-permute-done.8), channel_id=1, source_target_pairs={{0,1},{1,2},{2,3},{4,5},{5,6},{6,7},{8,9},{9,10},{10,11},{12,13},{... | collective-permute-start | bytes 3145736 | tf_op jit(solution)/shard_map/ppermute | solution.py:175
  377.4 39.5 %collective-permute-start.12 = (bf16[4,2,16,2,16,128]{5,4,3,2,1,0:T(8,128)(2,1)}, bf16[4,2,16,2,16,128]{5,4,3,2,1,0:T(8,128)(2,1)}, u32[]{:S(2)}, u32[]{:S(2)}) collective-permute-start(bf16[4,2,16,2,16,128]{5,4,3,2,1,0:T(8,128)(2,1)} %collective-permute-done.11), channel_id=1, source_target_pairs={{1,0},{2,1},{3,2},{5,4},{6,5},{7,6},{9,8},{10,9},{11,10},{13,12},{... | collective-permute-start | bytes 3145736 | tf_op jit(solution)/shard_map/ppermute | solution.py:176
  379.4 1.3 copy-start.4
  380.7 110.2 %all-to-all-start = ((bf16[16,2,128,256]{3,2,1,0:T(8,128)(2,1)}), bf16[16,2,128,256]{3,2,1,0:T(8,128)(2,1)}, u32[]{:S(2)}, u32[]{:S(2)}) async-start(bf16[16,2,128,256]{3,2,1,0:T(8,128)(2,1)} %get-tuple-element.10), calls=%async_computation | async-start | bytes 4194304 | tf_op jit(solution)/shard_map/all_to_all | solution.py:333
  394.4 23.9 %copy-start.6 = (bf16[8,1,16,2,16,128]{5,4,3,2,1,0:T(8,128)(2,1)S(1)}, bf16[8,1,16,2,16,128]{5,4,3,2,1,0:T(8,128)(2,1)}, u32[]{:S(2)}) copy-start(bf16[8,1,16,2,16,128]{5,4,3,2,1,0:T(8,128)(2,1)} %all-gather.12.cloned.1.call-done) | copy-start | bytes 3145732
  490.9 23.5 %copy-start.1 = (bf16[3,3,128,128]{3,2,1,0:T(8,128)(2,1)S(1)}, bf16[3,3,128,128]{3,2,1,0:T(8,128)(2,1)}, u32[]{:S(2)}) copy-start(bf16[3,3,128,128]{3,2,1,0:T(8,128)(2,1)} %param.6) | copy-start | bytes 884740
Sparse Core Ops, SparseCore 0:
  27.9 11.3 all-gather.9
  82.6 26.4 all-gather.11
  110.9 62.7 all-gather.17
  204.0 72.0 all-gather.15
  285.5 67.0 all-gather.13
